TPU v7x, 128 devices: a whole 4x4x4 slice. The times are simulated.
128 devices in a mesh: src: 8 (over y, z_lo), tgt: 16 (over x, z_hi, core).
Axes of the slice: x: 4, y: 4, z: 4 (z_hi: 2, z_lo: 2; z = z_hi * 2 + z_lo), core: 2. Of those that a mesh axis runs over, the one named last changes fastest.
Arguments:
- positions: float32 [3, 524288], P(None, ('src', 'tgt')), may hold values from -2.7 to 2.7
- velocities: float32 [3, 524288], P(None, ('src', 'tgt')), may hold values from -2.4 to 2.4
- accelerations: float32 [3, 524288], P(None, ('src', 'tgt')), may hold values from -6 to 6
- jerk_terms: float32 [3, 524288], P(None, ('src', 'tgt')), may hold values from -6 to 6
- masses: float32 [524288], P(('src', 'tgt')), may hold values from 5.722046e-07 to 5.722046e-06
- elapsed: float32 [524288], P(('src', 'tgt')), may hold values from 0.02 to 0.1
- active_idx: int32 [512], P(('src', 'tgt')), may hold values from 0 to 524287, as said below
- owners: int32 [512], P(('src', 'tgt')), may hold values from 0 to 7, as said below
- counts: int32 [512], P(('src', 'tgt')), may hold values from 1 to 16
- block_lists: int32 [512, 16], P(('src', 'tgt')), may hold values from 0 to 39, as said below
Outputs:
- new_states: float32 [6, 512], P(None, ('src', 'tgt'))
- fields: float32 [12, 512], P(None, ('src', 'tgt'))
- taylor: float32 [6, 512], P(None, ('src', 'tgt'))
Inputs may be any that keep to these rules, and one draw needn't show every extreme that they name: Entry i is a star of owner block owners[i] of its own group: with t = (i // 4) mod 16, (owners[i] 16 + t) * 4096 <= active_idx[i] < (owners[i] 16 + t + 1) * 4096. Entries are distinct. `owners`: among the 4 entries of one device at most 2 name the same owner; in each group some owner is named 2 times by every device of the group. `block_lists`: each row holds 16 distinct numbers; only the first counts[i] of row i are read.
All inputs are finite; a program needn't handle non-finite values.
Results may differ from a plain program's by a relative error of at most 0.0003.
Values sent between devices are 32-bit elements; how exact they have to be, the bound alone decides.
A program may use at most 64 MiB of HBM per device.

v0:
```python
import math

import jax
import jax.numpy as jnp
from jax import lax
from jax.sharding import PartitionSpec as P

BLOCK = 128
HALO_BLK = 4
SUBS = 2
CAP = 2


SOFTENING = 0.0001


def padded(block, sides, width):
    for axis, dim in sides:
        count = lax.axis_size(axis)
        forward = [(i, i + 1) for i in range(count - 1)]
        backward = [(target, source) for source, target in forward]
        low = lax.ppermute(
            lax.slice_in_dim(block, block.shape[dim] - width, None, axis=dim), axis, forward
        )
        high = lax.ppermute(lax.slice_in_dim(block, 0, width, axis=dim), axis, backward)
        block = jnp.concatenate([low, block, high], axis=dim)
    return block


def predict(position, velocity, acceleration, jerk_now, interval):
    new_position = position + interval * (
        velocity + interval * (0.5 * acceleration + interval * jerk_now / 6.0)
    )
    new_velocity = velocity + interval * (acceleration + 0.5 * interval * jerk_now)
    return (new_position, new_velocity)


def pair_terms(targets, sources):
    offset = sources[0:3] - targets[0:3, :, None]
    relative = sources[3:6] - targets[3:6, :, None]
    distance = offset[0] * offset[0] + offset[1] * offset[1] + offset[2] * offset[2] + SOFTENING
    inverse = lax.rsqrt(distance)
    weight = sources[6] * inverse * inverse * inverse
    radial = (
        3.0
        * (offset[0] * relative[0] + offset[1] * relative[1] + offset[2] * relative[2])
        / distance
    )
    pull_sum = jnp.sum(weight * offset, axis=-1)
    change = jnp.sum(weight * (relative - radial * offset), axis=-1)
    return jnp.concatenate([pull_sum, change], 0)


def source_field(targets, sources):
    source_count = sources.shape[1]
    wanted = 1 << max(9, 17 - (targets.shape[1] - 1).bit_length())
    tile_width = math.gcd(source_count, wanted)

    def accumulate(number, running):
        source_block = lax.dynamic_slice_in_dim(sources, number * tile_width, tile_width, 1)
        return running + pair_terms(targets, source_block[:, None, :])

    return lax.fori_loop(
        0, source_count // tile_width, accumulate, jnp.zeros((6, targets.shape[1]), jnp.float32)
    )


def correct(position, velocity, old_pull, old_change, new_pull, new_change, interval):
    jump = old_pull - new_pull
    snap_term = -6.0 * jump - interval * (4.0 * old_change + 2.0 * new_change)
    crackle = 12.0 * jump + 6.0 * interval * (old_change + new_change)
    new_position = position + interval * interval * (snap_term / 24.0 + crackle / 120.0)
    new_velocity = velocity + interval * (snap_term / 6.0 + crackle / 24.0)
    return (new_position, new_velocity, snap_term, crackle)


def neighbour_field(targets, nearby, usable, advance):
    moved_pos, moved_vel = predict(
        nearby[0:3], nearby[3:6], nearby[6:9], nearby[9:12], nearby[13] + advance[:, None]
    )
    sources = jnp.concatenate([moved_pos, moved_vel, (nearby[12] * usable)[None]], 0)
    return pair_terms(targets, sources)


def home_steps(nearby, usable, own_state, totals):
    interval = own_state[13]
    start_pos, start_vel = predict(
        own_state[0:3], own_state[3:6], own_state[6:9], own_state[9:12], interval
    )
    inner_field = neighbour_field(
        jnp.concatenate([start_pos, start_vel], 0), nearby, usable, jnp.zeros_like(interval)
    )
    regular = totals - inner_field
    position, velocity, snap_term, crackle = correct(
        start_pos, start_vel, own_state[6:9], own_state[9:12], totals[0:3], totals[3:6], interval
    )
    pull_now, change = (totals[0:3], totals[3:6])
    substep = 0.25 * interval
    for number in range(SUBS):
        advance = substep * (number + 1)
        guess_pos, guess_vel = predict(position, velocity, pull_now, change, substep)
        inner_field = neighbour_field(
            jnp.concatenate([guess_pos, guess_vel], 0), nearby, usable, advance
        )
        new_pull = regular[0:3] + advance * regular[3:6] + inner_field[0:3]
        new_change = regular[3:6] + inner_field[3:6]
        position, velocity, unused, ignored = correct(
            guess_pos, guess_vel, pull_now, change, new_pull, new_change, substep
        )
        pull_now, change = (new_pull, new_change)
    return jnp.concatenate([position, velocity, regular, inner_field, snap_term, crackle], 0)


def usable_mask(near_lists, near_counts, star_offset):
    lane_index = jnp.arange(BLOCK, dtype=jnp.int32)
    within = near_lists[:, :, None] * BLOCK + lane_index[None, None, :]
    listed = (
        jnp.arange(near_lists.shape[1], dtype=jnp.int32)[None, :, None] < near_counts[:, None, None]
    )
    itself = (star_offset + HALO_BLK * BLOCK)[:, None, None]
    return (listed & (within != itself)).reshape(near_lists.shape[0], -1).astype(jnp.float32)


def shards(
    positions,
    velocities,
    accelerations,
    jerk_terms,
    masses,
    elapsed,
    active_idx,
    owners,
    counts,
    block_lists,
):
    shard_len = positions.shape[1]
    src_size = lax.axis_size("src")
    tgt_size = lax.axis_size("tgt")
    raw_state = jnp.concatenate(
        [positions, velocities, accelerations, jerk_terms, masses[None], elapsed[None]], 0
    )
    pred_pos, pred_vel = predict(positions, velocities, accelerations, jerk_terms, elapsed)
    moving = jnp.concatenate([pred_pos, pred_vel], 0)
    sources = jnp.concatenate([moving, masses[None]], 0)
    first_star = (lax.axis_index("src") * tgt_size + lax.axis_index("tgt")) * shard_len
    group_idx = lax.all_gather(active_idx, "src", axis=0, tiled=True)
    offset = group_idx - first_star
    inside = (offset >= 0) & (offset < shard_len)
    picked = jnp.take(moving, jnp.clip(offset, 0, shard_len - 1), axis=1)
    group_targets = lax.psum(jnp.where(inside[None, :], picked, 0.0), "src")
    every = lax.all_gather(group_targets, "tgt", axis=1, tiled=True)
    ordered = every.reshape(6, tgt_size, src_size, -1).transpose(0, 2, 1, 3).reshape(6, -1)
    partial_value = source_field(ordered, sources)
    totals = lax.psum_scatter(partial_value, ("src", "tgt"), scatter_dimension=1, tiled=True)
    places = jnp.arange(active_idx.shape[0], dtype=jnp.int32)
    earlier = (owners[None, :] == owners[:, None]) & (places[None, :] < places[:, None])
    arrival = jnp.sum(earlier.astype(jnp.int32), axis=1)
    target_slot = owners * CAP + arrival
    slot_map = target_slot[:, None] == jnp.arange(src_size * CAP, dtype=jnp.int32)[None, :]
    slot_float = slot_map.astype(jnp.float32)
    send_float = jnp.dot(totals, slot_float, precision=lax.Precision.HIGHEST).reshape(
        6, src_size, CAP
    )
    details = jnp.concatenate([(active_idx % shard_len)[None], counts[None], block_lists.T], 0)
    send_int = jnp.sum(jnp.where(slot_map[None], details[:, :, None], 0), axis=1).reshape(
        -1, src_size, CAP
    )
    window = padded(raw_state, (("src", 1),), HALO_BLK * BLOCK)
    block_cells = window.reshape(14, -1, BLOCK)
    got_float = lax.all_to_all(send_float, "src", split_axis=1, concat_axis=1, tiled=True)
    got_int = lax.all_to_all(send_int, "src", split_axis=1, concat_axis=1, tiled=True)
    slot_width = got_float.shape[2]
    slot_totals = got_float.reshape(6, -1)
    details_here = got_int.reshape(got_int.shape[0], -1)
    star_offset = details_here[0]
    near_lists = details_here[2:].T
    nearby = jnp.take(block_cells, near_lists.reshape(-1), axis=1).reshape(
        14, near_lists.shape[0], -1
    )
    usable = usable_mask(near_lists, details_here[1], star_offset)
    own_state = jnp.take(raw_state, star_offset, axis=1)
    result = home_steps(nearby, usable, own_state, slot_totals)
    returned = lax.all_to_all(
        result.reshape(24, src_size, slot_width), "src", split_axis=1, concat_axis=1, tiled=True
    )
    result = jnp.dot(returned.reshape(24, -1), slot_float.T, precision=lax.Precision.HIGHEST)
    return (result[0:6], result[6:18], result[18:24])


def solution(mesh):
    in_specs = (
        P(None, ("src", "tgt")),
        P(None, ("src", "tgt")),
        P(None, ("src", "tgt")),
        P(None, ("src", "tgt")),
        P(("src", "tgt")),
        P(("src", "tgt")),
        P(("src", "tgt")),
        P(("src", "tgt")),
        P(("src", "tgt")),
        P(("src", "tgt"), None),
    )
    out_specs = (P(None, ("src", "tgt")), P(None, ("src", "tgt")), P(None, ("src", "tgt")))
    return jax.shard_map(shards, mesh=mesh, in_specs=in_specs, out_specs=out_specs, check_vma=False)
```

profile of v0, /device:TPU:0, one launch (start us, length us, event | category | flops | bytes accessed | tf_op | source)
XLA Modules:
  0.0 299.3 jit_solution(12398428150220140368)
XLA Ops:
  3.4 12.0 %all-reduce = s32[32]{0:T(128)S(1)} all-reduce(s32[32]{0:T(128)S(1)} %dynamic-update-slice), channel_id=1, replica_groups=mesh['src'=8,'tgt'=16] {'src'}, use_global_device_ids=true, to_apply=%add | all-reduce | flops 32 | bytes 256
  18.5 32.4 %psum.7 = f32[6,32]{0,1:T(8,128)S(1)} all-reduce(f32[6,32]{0,1:T(8,128)S(1)} %select_bitcast_fusion.1), channel_id=1, replica_groups=mesh['src'=8,'tgt'=16] {'src'}, use_global_device_ids=true, to_apply=%region_2.3 | all-reduce | flops 192 | bytes 1536 | tf_op jit(solution)/shard_map/psum | solution.py:150
  51.0 24.9 %all-gather = f32[16,32,6]{1,2,0:T(8,128)S(1)} all-gather(f32[1,32,6]{1,2,0:T(8,128)S(1)} %copy.332), channel_id=1, replica_groups=mesh['src'=8,'tgt'=16] {'tgt'}, dimensions={0}, use_global_device_ids=true | all-gather | bytes 13056 | tf_op jit(solution)/shard_map/all_gather | solution.py:151
  76.8 51.6 %while.14 = (s32[]{:T(128)}, f32[6,512]{1,0:T(8,128)S(1)}, f32[7,4096]{1,0:T(8,128)S(1)}, f32[6,512]{1,0:T(8,128)S(1)}, s32[]{:T(128)}, /*index=5*/s32[]{:T(128)}, s32[]{}, s32[]{:T(128)}, s32[]{:T(128)}, s32[]{}) while((s32[]{:T(128)}, f32[6,512]{1,0:T(8,128)S(1)}, f32[7,4096]{1,0:T(8,128)S(1)}, f32[6,512]{1,0:T(8,128)S(1)}, ...), condition=%wide.region_6.7_spmd.clone, body=%wide.region_3.6_spmd.clone.sunk | while | flops 12064777 | bytes 16931008 | solution.py:63
  79.2 2.7 fusion.39
  85.6 2.7 fusion.39
  92.1 2.7 fusion.39
  98.5 2.7 fusion.39
  105.0 2.7 fusion.39
  111.4 2.7 fusion.39
  117.9 2.7 fusion.39
  124.3 2.7 fusion.39
  128.4 62.3 %all-reduce.1 = f32[6,512]{1,0:T(8,128)S(1)} all-reduce(f32[6,512]{1,0:T(8,128)S(1)} %get-tuple-element.82), channel_id=2, replica_groups=mesh['src'=8,'tgt'=16] {'src','tgt'}, use_global_device_ids=true, to_apply=%region_7.8.clone | all-reduce | flops 3072 | bytes 24576
  193.1 3.6 %all-to-all-start.1 = ((f32[6,8,2]{0,2,1:T(2,128)}), f32[6,8,2]{0,2,1:T(2,128)S(1)}, u32[]{:S(2)}, u32[]{:S(2)}) async-start(f32[6,8,2]{0,2,1:T(2,128)} %bitcast.16), calls=%async_computation.1 | async-start | bytes 16384 | tf_op jit(solution)/shard_map/all_to_all | solution.py:170
  198.0 3.9 %collective-permute-start = (f32[14,512]{1,0:T(8,128)S(1)}, f32[14,512]{1,0:T(8,128)S(1)}, u32[]{:S(2)}, u32[]{:S(2)}) collective-permute-start(f32[14,512]{1,0:T(8,128)S(1)} %get-tuple-element.182), channel_id=1, source_target_pairs={{0,16},{16,32},{32,48},{48,64},{64,80},{80,96},{96,112},{1,17},{17... | collective-permute-start | bytes 86024 | tf_op jit(solution)/shard_map/ppermute | solution.py:22
  207.5 6.3 %all-to-all-start = ((s32[18,8,2]{0,2,1:T(2,128)}), s32[18,8,2]{0,2,1:T(2,128)S(1)}, u32[]{:S(2)}, u32[]{:S(2)}) async-start(s32[18,8,2]{0,2,1:T(2,128)} %bitcast.3), calls=%async_computation | async-start | bytes 16384 | tf_op jit(solution)/shard_map/all_to_all | solution.py:171
  214.7 5.3 %all-to-all-done = s32[18,8,2]{0,2,1:T(2,128)S(1)} async-done(((s32[18,8,2]{0,2,1:T(2,128)}), s32[18,8,2]{0,2,1:T(2,128)S(1)}, u32[]{:S(2)}, u32[]{:S(2)}) %all-to-all-start) | async-done | bytes 1184 | tf_op jit(solution)/shard_map/all_to_all | solution.py:171
  229.3 2.4 gather_fusion.2
  249.3 2.4 add_subtract_fusion.6
  260.0 3.3 %multiply_reduce_fusion.7 = (f32[3,256]{0,1:T(8,128)S(1)}, f32[3,256]{0,1:T(8,128)S(1)}) fusion(f32[256,128]{1,0:T(8,128)} %mul.1032, f32[3,256]{0,1:T(8,128)S(1)} %bitcast.100, f32[256,128]{1,0:T(8,128)S(1)} %bitcast.96, f32[14,256,128]{2,0,1:T(8,128)S(1)} %select_bitcast_fusion, f32[256,128]{1,0:T(8,128)} %mul.1053, f32[3,256]{0,1:T(8,128)S(1)} %bitcast.102, ...), kind=kLoop, calls=%fused_computation.28 | loop fusion | flops 1964544 | bytes 2109440 | tf_op jit(solution)/shard_map/reduce_sum | solution.py:49
  264.7 2.0 fusion.12
  270.6 3.3 %multiply_reduce_fusion.5 = (f32[3,256]{0,1:T(8,128)S(1)}, f32[3,256]{0,1:T(8,128)S(1)}) fusion(f32[256,128]{1,0:T(8,128)S(1)} %mul.1069, f32[3,256]{0,1:T(8,128)S(1)} %bitcast.101, f32[256,128]{1,0:T(8,128)} %get-tuple-element.187, f32[14,256,128]{2,0,1:T(8,128)S(1)} %select_bitcast_fusion, f32[256,128]{1,0:T(8,128)} %mul.1096, f32[3,256]{0,1:T(8,128)S(1)} %bitcast.103, ...), kind=kLoop, calls=%fused_computation.25 | loop fusion | flops 1964544 | bytes 2109440 | tf_op jit(solution)/shard_map/reduce_sum | solution.py:49
  285.6 3.0 %multiply_reduce_fusion.2 = (f32[3,256]{0,1:T(8,128)S(1)}, f32[3,256]{0,1:T(8,128)S(1)}) fusion(f32[256,128]{1,0:T(8,128)S(1)} %mul.1150, f32[3,256]{0,1:T(8,128)S(1)} %bitcast.99, f32[256,128]{1,0:T(8,128)S(1)} %copy-done.1, f32[256,128]{1,0:T(8,128)} %get-tuple-element.138, f32[256,128]{1,0:T(8,128)S(1)} %mul.1127, f32[3,256]{0,1:T(8,128)S(1)} %bitcast.98, ...), kind=kLoop, calls=%fused_computation.21 | loop fusion | flops 1964544 | bytes 2109440 | tf_op jit(solution)/shard_map/reduce_sum | solution.py:50
  289.2 8.5 %all_to_all.15 = f32[24,8,2]{0,2,1:T(2,128)S(1)} all-to-all(f32[24,8,2]{0,2,1:T(2,128)S(1)} %bitcast.116), channel_id=1, replica_groups=mesh['src'=8,'tgt'=16] {'src'}, dimensions={1} | all-to-all | bytes 3072 | tf_op jit(solution)/shard_map/all_to_all | solution.py:183
  (239 shorter events, 100.0 us)
Async XLA Ops:
  0.6 76.0 %copy-start.7 = (f32[4096]{0:T(1024)S(1)}, f32[4096]{0:T(1024)}, u32[]{:S(2)}) copy-start(f32[4096]{0:T(1024)} %param.16) | copy-start | bytes 49156
  76.7 120.0 %copy-start.3 = (f32[3,4096]{1,0:T(4,128)S(1)}, f32[3,4096]{1,0:T(4,128)}, u32[]{:S(2)}) copy-start(f32[3,4096]{1,0:T(4,128)} %param.12) | copy-start | bytes 147460
  76.7 120.0 %copy-start.4 = (f32[3,4096]{1,0:T(4,128)S(1)}, f32[3,4096]{1,0:T(4,128)}, u32[]{:S(2)}) copy-start(f32[3,4096]{1,0:T(4,128)} %param.13) | copy-start | bytes 147460
  76.7 120.0 %copy-start.5 = (f32[3,4096]{1,0:T(4,128)S(1)}, f32[3,4096]{1,0:T(4,128)}, u32[]{:S(2)}) copy-start(f32[3,4096]{1,0:T(4,128)} %param.14) | copy-start | bytes 147460
  76.8 120.0 %copy-start.6 = (f32[4096]{0:T(1024)S(1)}, f32[4096]{0:T(1024)}, u32[]{:S(2)}) copy-start(f32[4096]{0:T(1024)} %param.17) | copy-start | bytes 49156
  192.3 12.5 %copy-start.28 = (s32[4]{0:T(128)}, s32[4]{0:T(128)S(1)}, u32[]{:S(2)}) copy-start(s32[4]{0:T(128)S(1)} %multiply_add_fusion.14) | copy-start | bytes 52
  193.1 14.3 %all-to-all-start.1 = ((f32[6,8,2]{0,2,1:T(2,128)}), f32[6,8,2]{0,2,1:T(2,128)S(1)}, u32[]{:S(2)}, u32[]{:S(2)}) async-start(f32[6,8,2]{0,2,1:T(2,128)} %bitcast.16), calls=%async_computation.1 | async-start | bytes 16384 | tf_op jit(solution)/shard_map/all_to_all | solution.py:170
  198.0 31.1 %collective-permute-start = (f32[14,512]{1,0:T(8,128)S(1)}, f32[14,512]{1,0:T(8,128)S(1)}, u32[]{:S(2)}, u32[]{:S(2)}) collective-permute-start(f32[14,512]{1,0:T(8,128)S(1)} %get-tuple-element.182), channel_id=1, source_target_pairs={{0,16},{16,32},{32,48},{48,64},{64,80},{80,96},{96,112},{1,17},{17... | collective-permute-start | bytes 86024 | tf_op jit(solution)/shard_map/ppermute | solution.py:22
  201.9 27.2 %collective-permute-start.1 = (f32[14,512]{1,0:T(8,128)S(1)}, f32[14,512]{1,0:T(8,128)S(1)}, u32[]{:S(2)}, u32[]{:S(2)}) collective-permute-start(f32[14,512]{1,0:T(8,128)S(1)} %get-tuple-element.183), channel_id=1, source_target_pairs={{16,0},{32,16},{48,32},{64,48},{80,64},{96,80},{112,96},{17,1},{33... | collective-permute-start | bytes 86024 | tf_op jit(solution)/shard_map/ppermute | solution.py:25
  207.5 12.5 %all-to-all-start = ((s32[18,8,2]{0,2,1:T(2,128)}), s32[18,8,2]{0,2,1:T(2,128)S(1)}, u32[]{:S(2)}, u32[]{:S(2)}) async-start(s32[18,8,2]{0,2,1:T(2,128)} %bitcast.3), calls=%async_computation | async-start | bytes 16384 | tf_op jit(solution)/shard_map/all_to_all | solution.py:171
  222.0 9.6 %copy-start.17 = (f32[16]{0:T(128)}, f32[16]{0:T(128)S(1)}, u32[]{:S(2)}) copy-start(f32[16]{0:T(128)S(1)} %get-tuple-element.195) | copy-start | bytes 196
  222.8 8.9 %copy-start.13 = (f32[3,16]{1,0:T(4,128)}, f32[3,16]{1,0:T(4,128)S(1)}, u32[]{:S(2)}) copy-start(f32[3,16]{1,0:T(4,128)S(1)} %get-tuple-element.152) | copy-start | bytes 580
  222.8 8.9 %copy-start.15 = (f32[3,16]{1,0:T(4,128)}, f32[3,16]{1,0:T(4,128)S(1)}, u32[]{:S(2)}) copy-start(f32[3,16]{1,0:T(4,128)S(1)} %get-tuple-element.153) | copy-start | bytes 580
  222.8 8.8 %copy-start.12 = (f32[3,16]{1,0:T(4,128)}, f32[3,16]{1,0:T(4,128)S(1)}, u32[]{:S(2)}) copy-start(f32[3,16]{1,0:T(4,128)S(1)} %get-tuple-element.155) | copy-start | bytes 580
  222.8 26.5 %copy-start.8 = (f32[3,16]{1,0:T(4,128)}, f32[3,16]{1,0:T(4,128)S(1)}, u32[]{:S(2)}) copy-start(f32[3,16]{1,0:T(4,128)S(1)} %get-tuple-element.154) | copy-start | bytes 580
  251.7 8.3 %copy-start = (f32[1,256,128]{2,0,1:T(1,128)S(1)}, f32[1,256,128]{2,0,1:T(1,128)}, u32[]{:S(2)}) copy-start(f32[1,256,128]{2,0,1:T(1,128)} %get-tuple-element.166) | copy-start | bytes 393220
  274.0 11.6 %copy-start.1 = (f32[256,128]{1,0:T(8,128)S(1)}, f32[256,128]{1,0:T(8,128)}, u32[]{:S(2)}) copy-start(f32[256,128]{1,0:T(8,128)} %get-tuple-element.137) | copy-start | bytes 393220
  284.5 4.3 %copy-start.11 = (f32[3,16]{1,0:T(4,128)S(1)}, f32[3,16]{1,0:T(4,128)}, u32[]{:S(2)}) copy-start(f32[3,16]{1,0:T(4,128)} %get-tuple-element.141) | copy-start | bytes 580
  284.6 4.3 %copy-start.18 = (f32[16]{0:T(128)S(1)}, f32[16]{0:T(128)}, u32[]{:S(2)}) copy-start(f32[16]{0:T(128)} %copy-done.17) | copy-start | bytes 196
  284.6 4.3 %copy-start.10 = (f32[3,16]{1,0:T(4,128)S(1)}, f32[3,16]{1,0:T(4,128)}, u32[]{:S(2)}) copy-start(f32[3,16]{1,0:T(4,128)} %multiply_add_fusion.6) | copy-start | bytes 580
  284.6 4.3 %copy-start.24 = (f32[16]{0:T(128)S(1)}, f32[16]{0:T(128)}, u32[]{:S(2)}) copy-start(f32[16]{0:T(128)} %get-tuple-element.194) | copy-start | bytes 196
  284.6 4.3 %copy-start.14 = (f32[3,16]{1,0:T(4,128)S(1)}, f32[3,16]{1,0:T(4,128)}, u32[]{:S(2)}) copy-start(f32[3,16]{1,0:T(4,128)} %copy-done.13) | copy-start | bytes 580
  284.6 4.3 %copy-start.16 = (f32[3,16]{1,0:T(4,128)S(1)}, f32[3,16]{1,0:T(4,128)}, u32[]{:S(2)}) copy-start(f32[3,16]{1,0:T(4,128)} %copy-done.15) | copy-start | bytes 580
  284.7 13.1 %copy-start.29 = (s32[4]{0:T(128)S(1)}, s32[4]{0:T(128)}, u32[]{:S(2)}) copy-start(s32[4]{0:T(128)} %copy-done.28) | copy-start | bytes 52
  (10 other events, 22.8 us)
where the time goes:
time: 301 us; the launch traced here: 299 us
  blocking collectives  140 us (47%)
  other arithmetic  83 us (28%)
  local copies, waits for them, and re-layouts  52.4 us (17%)
  starting transfers between devices  15.2 us (5%)
  waiting for transfers between devices  5.28 us (2%)
    unnamed x2, blocking collectives  74.3 us
    psum x1, blocking collectives, shards(): group_targets = lax.psum(jnp.where(inside[None, :], picked, 0.0), 'src')  32.4 us
    all_gather x1, blocking collectives, shards(): every = lax.all_gather(group_targets, 'tgt', axis=1, tiled=True)  24.9 us
    mul x8, other arithmetic, pair_terms(): change = jnp.sum(weight * (relative - radial * offset), axis=-1)  21.2 us
    reduce_sum x11, other arithmetic, pair_terms(): pull_sum = jnp.sum(weight * offset, axis=-1)  17.7 us
    sub x8, other arithmetic, pair_terms(): relative = sources[3:6] - targets[3:6, :, None]  15.5 us
    all_to_all x1, blocking collectives, shards(): lax.all_to_all(result.reshape(24, src_size, slot_width), 'src', split_axi...  8.53 us
    all_to_all x1, starting transfers between devices, shards(): lax.all_to_all(send_int, 'src', split_axis=1, concat_axis=1, tiled=True)  6.34 us
  transfers between devices with their start and end apart: 4, of which 1 were waited for; matrix products, arithmetic and copies ran while one was open for 5% of the time, Pallas kernels for 0%

commit v1 on v0

v1 whole, which is shorter than its diff:
```python
import jax
import jax.numpy as jnp
from jax import lax
from jax.experimental import pallas as pl
from jax.experimental.pallas import tpu as pltpu
from jax.sharding import PartitionSpec as P

LANES = 128
ROWS = 8
BLOCK = 128
HALO = 4 * BLOCK
SUBS = 2
CAP = 2
ACT = 4
SRC = 8
TGT = 16
SOFTENING = 0.0001
MESH = pl.DeviceIdType.MESH
PAIRS = ((1, 0), (2, 0), (1, 1), (2, 1), (3, 1), (0, 1), (3, 0), (0, 0))
DX_TABLE = sum(dx * 4**at for at, (dx, dz) in enumerate(PAIRS))
DZ_TABLE = sum(dz * 2**at for at, (dx, dz) in enumerate(PAIRS))


def predict(position, velocity, acceleration, jerk_now, interval):
    new_position = [
        x + interval * (v + interval * (0.5 * a + interval * j / 6.0))
        for x, v, a, j in zip(position, velocity, acceleration, jerk_now)
    ]
    new_velocity = [
        v + interval * (a + 0.5 * interval * j)
        for v, a, j in zip(velocity, acceleration, jerk_now)
    ]
    return new_position, new_velocity


def correct(position, velocity, old_pull, old_change, new_pull, new_change, interval):
    new_position, new_velocity, snaps, crackles = [], [], [], []
    for x, v, a0, j0, a1, j1 in zip(
        position, velocity, old_pull, old_change, new_pull, new_change
    ):
        jump = a0 - a1
        snap = -6.0 * jump - interval * (4.0 * j0 + 2.0 * j1)
        crackle = 12.0 * jump + 6.0 * interval * (j0 + j1)
        new_position.append(x + interval * interval * (snap / 24.0 + crackle / 120.0))
        new_velocity.append(v + interval * (snap / 6.0 + crackle / 24.0))
        snaps.append(snap)
        crackles.append(crackle)
    return new_position, new_velocity, snaps, crackles


def pair_sums(sums, target, source, mass):
    u = [source[k] - target[k] for k in range(3)]
    e = [source[3 + k] - target[3 + k] for k in range(3)]
    distance = u[0] * u[0] + u[1] * u[1] + (u[2] * u[2] + SOFTENING)
    inverse = lax.rsqrt(distance)
    square = inverse * inverse
    weight = (mass * inverse) * square
    along = u[0] * e[0] + u[1] * e[1] + u[2] * e[2]
    radial = weight * (along * square)
    return (
        [sums[k] + weight * u[k] for k in range(3)]
        + [sums[3 + k] + weight * e[k] for k in range(3)]
        + [sums[6 + k] + radial * u[k] for k in range(3)]
    )


def total_of(sums):
    six = sums[0:3] + [sums[3 + k] - 3.0 * sums[6 + k] for k in range(3)]
    return [
        jnp.broadcast_to(jnp.sum(part, axis=1, keepdims=True), (ROWS, LANES)) for part in six
    ]


def lane_of(tile, lane):
    return jnp.broadcast_to(tile[:, lane : lane + 1], (ROWS, LANES))


def row_of(ref, row, block):
    lanes = pl.ds(pl.multiple_of(block * LANES, LANES), LANES)
    return jnp.broadcast_to(ref[row : row + 1, lanes], (ROWS, LANES))


def kernel(
    pos, vel, acc, jrk, mas, ela, idx, own, cnt, lists,
    o_state, o_fields, o_taylor,
    wpos, wvel, wacc, wjrk, wmas, wela, ppos, pvel, mw,
    s1b, s1r, s2b, s2r, s3b, s3r, s4b, s4r, s5b, s5r, s6b, s6r,
    load_sem, halo_send, halo_recv, src_send, src_recv, tgt_send, tgt_recv, sum_send, sum_recv,
):
    stars = pos.shape[1]
    blocks = stars // BLOCK
    window_blocks = wpos.shape[1] // BLOCK
    me = lax.axis_index("src")
    my_group = lax.axis_index("tgt")
    my_x, my_z, my_core = my_group // 4, (my_group // 2) % 2, my_group % 2

    def src_peer(step):
        return {"src": lax.rem(me + step, SRC)}

    def tgt_peer(dx, dz, dc):
        x, z, core = lax.rem(my_x + dx, 4), lax.rem(my_z + dz, 2), lax.rem(my_core + dc, 2)
        return {"tgt": x * 4 + z * 2 + core}

    def tile_rows(at):
        return pl.ds(pl.multiple_of(at * ROWS, ROWS), ROWS)

    lane = lax.broadcasted_iota(jnp.int32, (ROWS, LANES), 1)
    sub = lax.broadcasted_iota(jnp.int32, (ROWS, LANES), 0)
    zero = jnp.zeros((ROWS, LANES), jnp.float32)

    arrays = ((pos, wpos), (vel, wvel), (acc, wacc), (jrk, wjrk), (mas, wmas), (ela, wela))
    loads = [
        pltpu.make_async_copy(hbm, win.at[:, HALO : HALO + stars], load_sem.at[at])
        for at, (hbm, win) in enumerate(arrays)
    ]
    for load in loads:
        load.start()

    barrier = pltpu.get_barrier_semaphore()
    for step in range(1, SRC):
        pl.semaphore_signal(barrier, inc=1, device_id=src_peer(step), device_id_type=MESH)
    for at in range(1, TGT):
        pl.semaphore_signal(
            barrier,
            inc=1,
            device_id=tgt_peer(at // 4, (at // 2) % 2, at % 2),
            device_id_type=MESH,
        )

    tile = jnp.zeros((ROWS, LANES), jnp.int32)
    for place in range(ACT):
        for at, ref in enumerate((idx, own, cnt)):
            tile = jnp.where((sub == place) & (lane == 16 + at), ref[place], tile)
    s1b[...] = tile
    s1b[0:ACT, 0:16] = lists[...]

    pl.semaphore_wait(barrier, SRC + TGT - 2)

    def share(stage, sent, landed):
        copies = []
        for step in range(1, SRC):
            copies.append(
                pltpu.make_async_remote_copy(
                    src_ref=sent,
                    dst_ref=landed.at[tile_rows(me), :],
                    send_sem=src_send.at[stage, step],
                    recv_sem=src_recv.at[stage, step],
                    device_id=src_peer(step),
                    device_id_type=MESH,
                )
            )
        for copy in copies:
            copy.start()
        return copies

    first = share(0, s1b, s1r)
    s1r[tile_rows(me), :] = s1b[...]

    up = [
        pltpu.make_async_remote_copy(
            src_ref=hbm.at[:, stars - HALO : stars],
            dst_ref=win.at[:, 0:HALO],
            send_sem=halo_send.at[0, at],
            recv_sem=halo_recv.at[0, at],
            device_id={"src": lax.rem(me + 1, SRC)},
            device_id_type=MESH,
        )
        for at, (hbm, win) in enumerate(arrays)
    ]
    down = [
        pltpu.make_async_remote_copy(
            src_ref=hbm.at[:, 0:HALO],
            dst_ref=win.at[:, HALO + stars : 2 * HALO + stars],
            send_sem=halo_send.at[1, at],
            recv_sem=halo_recv.at[1, at],
            device_id={"src": lax.rem(me + SRC - 1, SRC)},
            device_id_type=MESH,
        )
        for at, (hbm, win) in enumerate(arrays)
    ]

    @pl.when(me < SRC - 1)
    def _():
        for copy in up:
            copy.start()

    @pl.when(me > 0)
    def _():
        for copy in down:
            copy.start()

    @pl.when(me == 0)
    def _():
        for hbm, win in arrays:
            win[:, 0:HALO] = jnp.zeros((win.shape[0], HALO), jnp.float32)

    @pl.when(me == SRC - 1)
    def _():
        for hbm, win in arrays:
            win[:, HALO + stars :] = jnp.zeros((win.shape[0], HALO), jnp.float32)

    for load in loads:
        load.wait()

    chunk = 4 * LANES

    def predict_chunk(at, carry):
        here = pl.ds(pl.multiple_of(at * chunk, LANES), chunk)
        there = pl.ds(pl.multiple_of(HALO + at * chunk, LANES), chunk)
        (moved,), (speed,) = predict(
            [wpos[:, there]], [wvel[:, there]], [wacc[:, there]], [wjrk[:, there]], wela[:, there]
        )
        ppos[:, here] = moved
        pvel[:, here] = speed
        return carry

    lax.fori_loop(0, stars // chunk, predict_chunk, 0)

    for copy in first:
        copy.wait_recv()

    numbers = [s1r[pl.ds(place, SRC, stride=ROWS), :] for place in range(ACT)]
    chosen = [[], []]
    before = jnp.zeros((ROWS, LANES), jnp.int32)
    for place in range(ACT):
        mine = lane_of(numbers[place], 17) == me
        for c in range(CAP):
            chosen[c].append(mine & (before == c))
        before = before + jnp.where(mine, 1, 0)

    def pick(c, values, empty):
        result = empty
        for place in range(ACT):
            result = jnp.where(chosen[c][place], values[place], result)
        return result

    izero = jnp.zeros((ROWS, LANES), jnp.int32)
    detail = [pick(c, numbers, izero) for c in range(CAP)]
    first_star = (me * TGT + my_group) * stars
    offset = [lane_of(detail[c], 16) - first_star for c in range(CAP)]
    count = [lane_of(detail[c], 18) for c in range(CAP)]

    def extract(refs, base):
        wide = sum(ref.shape[0] for ref in refs)

        def step(block, found):
            rows = [
                row_of(ref, row, block + base) for ref in refs for row in range(ref.shape[0])
            ]
            out = []
            for c in range(CAP):
                here = lane + block * BLOCK == offset[c]
                out.append([jnp.where(here, row, old) for row, old in zip(rows, found[c])])
            return out

        found = lax.fori_loop(0, blocks, step, [[zero] * wide for _ in range(CAP)], unroll=2)
        return [
            [
                jnp.broadcast_to(jnp.sum(part, axis=1, keepdims=True), (ROWS, LANES))
                for part in found[c]
            ]
            for c in range(CAP)
        ]

    start = extract((ppos, pvel), 0)

    def spread(values, width):
        slots = []
        for c in range(CAP):
            slot = zero
            for k, value in enumerate(values[c]):
                slot = jnp.where(lax.rem(lane, width) == k, value, slot)
            slots.append(slot)
        result = zero
        for place in range(ACT):
            there = lane // width == place
            for c in range(CAP):
                result = jnp.where(there & chosen[c][place], slots[c], result)
        return result

    s2b[...] = spread(start, 8)
    second = share(1, s2b, s2r)
    s2r[tile_rows(me), :] = s2b[...]

    raw = extract((wpos, wvel, wacc, wjrk, wela), HALO // BLOCK)

    def mask_block(block, carry):
        mass = row_of(wmas, 0, block)
        for c in range(CAP):
            listed = jnp.where((detail[c] == block) & (lane < count[c]), 1.0, 0.0)
            member = jnp.broadcast_to(jnp.sum(listed, axis=1, keepdims=True), (ROWS, LANES))
            itself = lane + block * BLOCK == offset[c] + HALO
            mw[block, c] = jnp.where(itself, 0.0, member * mass)
        return carry

    @pl.when(me > 0)
    def _():
        for copy in up:
            copy.wait_recv()

    @pl.when(me < SRC - 1)
    def _():
        for copy in down:
            copy.wait_recv()

    lax.fori_loop(0, window_blocks, mask_block, 0, unroll=4)

    for copy in second:
        copy.wait_recv()

    def gathered(ref):
        total = ref[0:ROWS, :]
        for at in range(1, SRC):
            total = total + ref[at * ROWS : (at + 1) * ROWS, :]
        return total

    group_targets = gathered(s2r)
    s3b[...] = group_targets
    s3r[0] = group_targets
    third = []
    for dx, dz in PAIRS:
        for dc in (1, 0):
            if (dx, dz, dc) == (0, 0, 0):
                continue
            there = ((4 - dx) % 4) * 4 + dz * 2 + dc
            third.append(
                pltpu.make_async_remote_copy(
                    src_ref=s3b,
                    dst_ref=s3r.at[there],
                    send_sem=tgt_send.at[there],
                    recv_sem=tgt_recv.at[there],
                    device_id=tgt_peer(dx, dz, dc),
                    device_id_type=MESH,
                )
            )
    for copy in third:
        copy.start()

    def near_field(targets, advance):
        def step(block, sums):
            x = [row_of(wpos, k, block) for k in range(3)]
            v = [row_of(wvel, k, block) for k in range(3)]
            a = [row_of(wacc, k, block) for k in range(3)]
            j = [row_of(wjrk, k, block) for k in range(3)]
            since = row_of(wela, 0, block)
            out = []
            for c in range(CAP):
                moved, speed = predict(x, v, a, j, since + advance[c])
                out.append(pair_sums(sums[c], targets[c], moved + speed, mw[block, c]))
            return out

        sums = lax.fori_loop(0, window_blocks, step, [[zero] * 9 for _ in range(CAP)], unroll=2)
        return [total_of(sums[c]) for c in range(CAP)]

    inner = near_field(start, [zero] * CAP)

    def field(targets):
        result = zero
        for half in range(2):
            places = (2 * half, 2 * half + 1)
            aims = [[lane_of(targets, place * 8 + k) for k in range(6)] for place in places]

            def step(block, sums):
                source = [row_of(ppos, k, block) for k in range(3)]
                source += [row_of(pvel, k, block) for k in range(3)]
                mass = row_of(wmas, 0, block + HALO // BLOCK)
                return [pair_sums(sums[at], aims[at], source, mass) for at in range(2)]

            sums = lax.fori_loop(0, blocks, step, [[zero] * 9 for _ in range(2)], unroll=2)
            for at, place in enumerate(places):
                for k, value in enumerate(total_of(sums[at])):
                    result = jnp.where(lane == place * 8 + k, value, result)
        return result

    def sum_copy(at, dx, dz, dc):
        there = lax.rem(4 - dx, 4) * 4 + dz * 2 + dc
        return pltpu.make_async_remote_copy(
            src_ref=s4b.at[at],
            dst_ref=s4r.at[there],
            send_sem=sum_send.at[at],
            recv_sem=sum_recv.at[there],
            device_id=tgt_peer(dx, dz, dc),
            device_id_type=MESH,
        )

    def group_pair(pair, tables):
        dx, dz = lax.rem(tables[0], 4), lax.rem(tables[1], 2)
        for dc in (1, 0):
            at = dx * 4 + dz * 2 + dc

            def wait():
                pltpu.make_async_remote_copy(
                    src_ref=s3b,
                    dst_ref=s3r.at[at],
                    send_sem=tgt_send.at[at],
                    recv_sem=tgt_recv.at[at],
                    device_id=tgt_peer(dx, dz, dc),
                    device_id_type=MESH,
                ).wait_recv()

            if dc:
                wait()
            else:
                pl.when(pair < len(PAIRS) - 1)(wait)
            result = field(s3r[at])

            def send():
                s4b[at] = result
                sum_copy(at, dx, dz, dc).start()

            if dc:
                send()
            else:
                pl.when(pair < len(PAIRS) - 1)(send)

                @pl.when(pair == len(PAIRS) - 1)
                def _():
                    s4r[0] = result

        return tables[0] // 4, tables[1] // 2

    lax.fori_loop(0, len(PAIRS), group_pair, (jnp.int32(DX_TABLE), jnp.int32(DZ_TABLE)))

    for at in range(1, TGT):
        sum_copy(at, at // 4, (at // 2) % 2, at % 2).wait_send()
        pltpu.make_async_remote_copy(
            src_ref=s4b.at[at],
            dst_ref=s4r.at[at],
            send_sem=sum_send.at[at],
            recv_sem=sum_recv.at[at],
            device_id=tgt_peer(at // 4, (at // 2) % 2, at % 2),
            device_id_type=MESH,
        ).wait_recv()
    group_sum = s4r[0]
    for at in range(1, TGT):
        group_sum = group_sum + s4r[at]

    s5b[...] = group_sum
    fifth = share(2, s5b, s5r)
    s5r[tile_rows(me), :] = group_sum
    for copy in fifth:
        copy.wait_recv()
    summed = gathered(s5r)
    lanes_of = [[lane_of(summed, place * 8 + k) for place in range(ACT)] for k in range(6)]

    totals = [[pick(c, lanes_of[k], zero) for k in range(6)] for c in range(CAP)]
    states = []
    for c in range(CAP):
        interval = raw[c][12]
        old_pull, old_change = raw[c][6:9], raw[c][9:12]
        regular = [totals[c][k] - inner[c][k] for k in range(6)]
        x, v, snap, crackle = correct(
            start[c][0:3],
            start[c][3:6],
            old_pull,
            old_change,
            totals[c][0:3],
            totals[c][3:6],
            interval,
        )
        states.append((x, v, totals[c][0:3], totals[c][3:6], 0.25 * interval, regular, snap + crackle))
    for number in range(SUBS):
        advance = [states[c][4] * (number + 1) for c in range(CAP)]
        guesses = [predict(*states[c][0:5]) for c in range(CAP)]
        inner = near_field([x + v for x, v in guesses], advance)
        after = []
        for c in range(CAP):
            x, v, pull, change, substep, regular, rest = states[c]
            new_pull = [
                regular[k] + advance[c] * regular[3 + k] + inner[c][k] for k in range(3)
            ]
            new_change = [regular[3 + k] + inner[c][3 + k] for k in range(3)]
            x, v, unused, ignored = correct(
                guesses[c][0], guesses[c][1], pull, change, new_pull, new_change, substep
            )
            after.append((x, v, new_pull, new_change, substep, regular, rest))
        states = after

    results = [
        states[c][0] + states[c][1] + states[c][5] + inner[c] + states[c][6] for c in range(CAP)
    ]
    s6b[...] = spread(results, 32)
    sixth = share(3, s6b, s6r)
    s6r[tile_rows(me), :] = s6b[...]
    for copy in sixth:
        copy.wait_recv()
    mine = jnp.sum(s6r[pl.ds(me, SRC, stride=ROWS), :], axis=0, keepdims=True)
    mine = jnp.broadcast_to(mine, (ROWS, LANES))
    shifted = mine
    for place in range(1, ACT):
        shifted = jnp.where(sub == place, pltpu.roll(mine, LANES - 32 * place, 1), shifted)
    columns = jnp.transpose(shifted)
    o_state[...] = columns[0:6, 0:ACT]
    o_fields[...] = columns[6:18, 0:ACT]
    o_taylor[...] = columns[18:24, 0:ACT]

    for copy in first + second + third + fifth + sixth:
        copy.wait_send()

    @pl.when(me < SRC - 1)
    def _():
        for copy in up:
            copy.wait_send()

    @pl.when(me > 0)
    def _():
        for copy in down:
            copy.wait_send()


def shards(
    positions,
    velocities,
    accelerations,
    jerk_terms,
    masses,
    elapsed,
    active_idx,
    owners,
    counts,
    block_lists,
):
    stars = positions.shape[1]
    window = stars + 2 * HALO
    hbm = pl.BlockSpec(memory_space=pl.ANY)
    smem = pl.BlockSpec(memory_space=pltpu.SMEM)
    vmem = pl.BlockSpec(memory_space=pltpu.VMEM)
    tile = pltpu.VMEM((ROWS, LANES), jnp.float32)
    landed = pltpu.VMEM((SRC * ROWS, LANES), jnp.float32)
    groups = pltpu.VMEM((TGT, ROWS, LANES), jnp.float32)
    itile = pltpu.VMEM((ROWS, LANES), jnp.int32)
    ilanded = pltpu.VMEM((SRC * ROWS, LANES), jnp.int32)
    three = pltpu.VMEM((3, window), jnp.float32)
    one = pltpu.VMEM((1, window), jnp.float32)
    predicted = pltpu.VMEM((3, stars), jnp.float32)
    dma = pltpu.SemaphoreType.DMA
    return pl.pallas_call(
        kernel,
        out_shape=(
            jax.ShapeDtypeStruct((6, ACT), jnp.float32),
            jax.ShapeDtypeStruct((12, ACT), jnp.float32),
            jax.ShapeDtypeStruct((6, ACT), jnp.float32),
        ),
        in_specs=[hbm] * 6 + [smem] * 3 + [vmem],
        out_specs=(vmem, vmem, vmem),
        scratch_shapes=[
            three, three, three, three, one, one, predicted, predicted,
            pltpu.VMEM((window // BLOCK, CAP, ROWS, LANES), jnp.float32),
            itile, ilanded, tile, landed, tile, groups, groups, groups, tile, landed, tile, landed,
            dma((6,)), dma((2, 6)), dma((2, 6)), dma((4, SRC)), dma((4, SRC)),
            dma((TGT,)), dma((TGT,)), dma((TGT,)), dma((TGT,)),
        ],
        compiler_params=pltpu.CompilerParams(collective_id=0, has_side_effects=True),
    )(
        positions,
        velocities,
        accelerations,
        jerk_terms,
        masses[None],
        elapsed[None],
        active_idx,
        owners,
        counts,
        block_lists,
    )


def solution(mesh):
    in_specs = (
        P(None, ("src", "tgt")),
        P(None, ("src", "tgt")),
        P(None, ("src", "tgt")),
        P(None, ("src", "tgt")),
        P(("src", "tgt")),
        P(("src", "tgt")),
        P(("src", "tgt")),
        P(("src", "tgt")),
        P(("src", "tgt")),
        P(("src", "tgt"), None),
    )
    out_specs = (P(None, ("src", "tgt")), P(None, ("src", "tgt")), P(None, ("src", "tgt")))
    return jax.shard_map(shards, mesh=mesh, in_specs=in_specs, out_specs=out_specs, check_vma=False)
```

time: 301 us -> 54.7 us (0.18)
  blocking collectives: 140 us -> 0 us
  other arithmetic: 83 us -> 0 us
  Pallas kernels: 0 us -> 51.2 us
  local copies, waits for them, and re-layouts: 52.4 us -> 2.68 us
  starting transfers between devices: 15.2 us -> 0 us
  waiting for transfers between devices: 5.28 us -> 0 us
    unnamed x2 -> x0, blocking collectives: 74.3 us -> none
    pallas_call x0 -> x1, Pallas kernels: none -> 51.2 us  [shards(): pl.pallas_call(kernel, out_shape=(jax.ShapeDtypeStruct((6, ACT), jnp.floa...]
    psum x1 -> x0, blocking collectives: 32.4 us -> none  [shards(): group_targets = lax.psum(jnp.where(inside[None, :], picked, 0.0), 'src')]
    mul x16 -> x0, other arithmetic: 27.3 us -> none  [the longest x8 21.2 us: pair_terms(): change = jnp.sum(weight * (relative - radial * offset), axis=-1)]
    all_gather x1 -> x0, blocking collectives: 24.9 us -> none  [shards(): every = lax.all_gather(group_targets, 'tgt', axis=1, tiled=True)]
    reduce_sum x17 -> x0, other arithmetic: 23 us -> none  [the longest x11 17.7 us: pair_terms(): pull_sum = jnp.sum(weight * offset, axis=-1)]
    sub x19 -> x0, other arithmetic: 22.1 us -> none  [the longest x8 15.5 us: pair_terms(): relative = sources[3:6] - targets[3:6, :, None]]
    slice x34 -> x0, local copies, waits for them, and re-layouts: 16.4 us -> none  [the longest x2 3.62 us: neighbour_field(): nearby[9:12]]
  transfers between devices with their start and end apart: 4 -> 0, of which waited for: 1 -> 0; matrix products, arithmetic and copies ran while one was open for 5% -> 0% of each run, Pallas kernels for 0% -> 0%
where the time goes in v1:
time: 54.7 us; the launch traced here: 54.5 us
  Pallas kernels  51.2 us (94%)
  local copies, waits for them, and re-layouts  2.68 us (5%)
  between operations  0.65 us (1%)
    pallas_call x1, Pallas kernels, shards(): pl.pallas_call(kernel, out_shape=(jax.ShapeDtypeStruct((6, ACT), jnp.floa...  51.2 us
    pallas_call x3, local copies, waits for them, and re-layouts, shards(): pl.pallas_call(kernel, out_shape=(jax.ShapeDtypeStruct((6, ACT), jnp.floa...  2.66 us

profile of v1, /device:TPU:0, one launch (start us, length us, event | category | flops | bytes accessed | tf_op | source)
XLA Modules:
  0.0 54.5 jit_solution(14686694625901038237)
XLA Ops:
  0.6 51.2 %shard_map.121 = (f32[6,4]{1,0:T(8,128)}, f32[12,4]{1,0:T(8,128)}, f32[6,4]{1,0:T(8,128)}) custom-call(f32[3,4096]{1,0:T(4,128)} %pos.1, f32[3,4096]{1,0:T(4,128)} %vel.1, f32[3,4096]{1,0:T(4,128)} %acc.1, f32[3,4096]{1,0:T(4,128)} %jrk.1, f32[1,4096]{1,0:T(1,128)} %bitcast.2, f32[1,4096]{1,0:T(1,128)} %bitcast.3, s32[4]{0:T(128)} %idx.1, s32[4]{0:T(128)} %own.1, ...), custom_call_target="tpu_custom_call" | custom-call | tf_op jit(solution)/shard_map/pallas_call | solution.py:537
  51.8 0.0 copy-start
  51.9 1.3 %copy.13 = f32[6,4]{0,1:T(4,128)} copy(f32[6,4]{1,0:T(8,128)} %get-tuple-element.3) | data formatting | bytes 192 | tf_op jit(solution)/shard_map/pallas_call | solution.py:537
  53.2 0.0 copy-done
  53.2 0.0 copy-start.1
  53.2 0.7 %copy.14 = f32[12,4]{0,1:T(4,128)} copy(f32[12,4]{1,0:T(8,128)S(1)} %copy-done) | data formatting | bytes 384 | tf_op jit(solution)/shard_map/pallas_call | solution.py:537
  53.9 0.0 copy-done.1
  53.9 0.7 %copy.15 = f32[6,4]{0,1:T(4,128)} copy(f32[6,4]{1,0:T(8,128)S(1)} %copy-done.1) | data formatting | bytes 192 | tf_op jit(solution)/shard_map/pallas_call | solution.py:537
Async XLA Ops:
  51.8 1.3 %copy-start = (f32[12,4]{1,0:T(8,128)S(1)}, f32[12,4]{1,0:T(8,128)}, u32[]{:S(2)}) copy-start(f32[12,4]{1,0:T(8,128)} %get-tuple-element.4) | copy-start | bytes 580
  53.2 0.7 %copy-start.1 = (f32[6,4]{1,0:T(8,128)S(1)}, f32[6,4]{1,0:T(8,128)}, u32[]{:S(2)}) copy-start(f32[6,4]{1,0:T(8,128)} %get-tuple-element.5) | copy-start | bytes 292

commit v2 on v1

--- a/solution.py
+++ b/solution.py
@@ -55,12 +55,12 @@
     inverse = lax.rsqrt(distance)
     square = inverse * inverse
     weight = (mass * inverse) * square
-    along = u[0] * e[0] + u[1] * e[1] + u[2] * e[2]
-    radial = weight * (along * square)
+    radial = (u[0] * e[0] + u[1] * e[1] + u[2] * e[2]) * square
+    pull = [weight * u[k] for k in range(3)]
     return (
-        [sums[k] + weight * u[k] for k in range(3)]
+        [sums[k] + pull[k] for k in range(3)]
         + [sums[3 + k] + weight * e[k] for k in range(3)]
-        + [sums[6 + k] + radial * u[k] for k in range(3)]
+        + [sums[6 + k] + radial * pull[k] for k in range(3)]
     )
 
 
@@ -82,8 +82,8 @@
 
 def kernel(
     pos, vel, acc, jrk, mas, ela, idx, own, cnt, lists,
-    o_state, o_fields, o_taylor,
-    wpos, wvel, wacc, wjrk, wmas, wela, ppos, pvel, mw,
+    o_all,
+    wpos, wvel, wacc, wjrk, wmas, wela, ppos, pvel, mw, moved,
     s1b, s1r, s2b, s2r, s3b, s3r, s4b, s4r, s5b, s5r, s6b, s6r,
     load_sem, halo_send, halo_recv, src_send, src_recv, tgt_send, tgt_recv, sum_send, sum_recv,
 ):
@@ -205,16 +205,15 @@
     chunk = 4 * LANES
 
     def predict_chunk(at, carry):
-        here = pl.ds(pl.multiple_of(at * chunk, LANES), chunk)
-        there = pl.ds(pl.multiple_of(HALO + at * chunk, LANES), chunk)
-        (moved,), (speed,) = predict(
+        there = pl.ds(pl.multiple_of(at * chunk, LANES), chunk)
+        (place,), (speed,) = predict(
             [wpos[:, there]], [wvel[:, there]], [wacc[:, there]], [wjrk[:, there]], wela[:, there]
         )
-        ppos[:, here] = moved
-        pvel[:, here] = speed
+        ppos[:, there] = place
+        pvel[:, there] = speed
         return carry
 
-    lax.fori_loop(0, stars // chunk, predict_chunk, 0)
+    lax.fori_loop(1, 1 + stars // chunk, predict_chunk, 0)
 
     for copy in first:
         copy.wait_recv()
@@ -240,12 +239,12 @@
     offset = [lane_of(detail[c], 16) - first_star for c in range(CAP)]
     count = [lane_of(detail[c], 18) for c in range(CAP)]
 
-    def extract(refs, base):
+    def extract(refs):
         wide = sum(ref.shape[0] for ref in refs)
 
         def step(block, found):
             rows = [
-                row_of(ref, row, block + base) for ref in refs for row in range(ref.shape[0])
+                row_of(ref, row, block + HALO // BLOCK) for ref in refs for row in range(ref.shape[0])
             ]
             out = []
             for c in range(CAP):
@@ -262,7 +261,7 @@
             for c in range(CAP)
         ]
 
-    start = extract((ppos, pvel), 0)
+    start = extract((ppos, pvel))
 
     def spread(values, width):
         slots = []
@@ -282,7 +281,7 @@
     second = share(1, s2b, s2r)
     s2r[tile_rows(me), :] = s2b[...]
 
-    raw = extract((wpos, wvel, wacc, wjrk, wela), HALO // BLOCK)
+    raw = extract((wpos, wvel, wacc, wjrk, wela))
 
     def mask_block(block, carry):
         mass = row_of(wmas, 0, block)
@@ -336,23 +335,42 @@
     for copy in third:
         copy.start()
 
-    def near_field(targets, advance):
+    def advance_block(block, carry):
+        x = [row_of(wpos, k, block) for k in range(3)]
+        v = [row_of(wvel, k, block) for k in range(3)]
+        a = [row_of(wacc, k, block) for k in range(3)]
+        half = [0.5 * row for row in a]
+        j = [row_of(wjrk, k, block) for k in range(3)]
+        sixth_j = [row / 6.0 for row in j]
+        half_j = [0.5 * row for row in j]
+        since = row_of(wela, 0, block)
+        for number in range(SUBS):
+            for c in range(CAP):
+                d = since + (0.25 * (number + 1)) * raw[c][12]
+                for k in range(3):
+                    moved[number, block, c, k] = x[k] + d * (
+                        v[k] + d * (half[k] + d * sixth_j[k])
+                    )
+                    moved[number, block, c, 3 + k] = v[k] + d * (a[k] + d * half_j[k])
+        return carry
+
+    lax.fori_loop(0, window_blocks, advance_block, 0)
+
+    def near_field(targets, number):
         def step(block, sums):
-            x = [row_of(wpos, k, block) for k in range(3)]
-            v = [row_of(wvel, k, block) for k in range(3)]
-            a = [row_of(wacc, k, block) for k in range(3)]
-            j = [row_of(wjrk, k, block) for k in range(3)]
-            since = row_of(wela, 0, block)
-            out = []
-            for c in range(CAP):
-                moved, speed = predict(x, v, a, j, since + advance[c])
-                out.append(pair_sums(sums[c], targets[c], moved + speed, mw[block, c]))
-            return out
-
-        sums = lax.fori_loop(0, window_blocks, step, [[zero] * 9 for _ in range(CAP)], unroll=2)
+            if number is None:
+                source = [row_of(ref, k, block) for ref in (ppos, pvel) for k in range(3)]
+                sources = [source] * CAP
+            else:
+                sources = [[moved[number, block, c, k] for k in range(6)] for c in range(CAP)]
+            return [pair_sums(sums[c], targets[c], sources[c], mw[block, c]) for c in range(CAP)]
+
+        sums = lax.fori_loop(0, window_blocks, step, [[zero] * 9 for _ in range(CAP)], unroll=8)
         return [total_of(sums[c]) for c in range(CAP)]
 
-    inner = near_field(start, [zero] * CAP)
+    predict_chunk(0, 0)
+    predict_chunk(window_blocks * LANES // chunk - 1, 0)
+    inner = near_field(start, None)
 
     def field(targets):
         result = zero
@@ -363,10 +381,16 @@
             def step(block, sums):
                 source = [row_of(ppos, k, block) for k in range(3)]
                 source += [row_of(pvel, k, block) for k in range(3)]
-                mass = row_of(wmas, 0, block + HALO // BLOCK)
+                mass = row_of(wmas, 0, block)
                 return [pair_sums(sums[at], aims[at], source, mass) for at in range(2)]
 
-            sums = lax.fori_loop(0, blocks, step, [[zero] * 9 for _ in range(2)], unroll=2)
+            sums = lax.fori_loop(
+                HALO // BLOCK,
+                HALO // BLOCK + blocks,
+                step,
+                [[zero] * 9 for _ in range(2)],
+                unroll=8,
+            )
             for at, place in enumerate(places):
                 for k, value in enumerate(total_of(sums[at])):
                     result = jnp.where(lane == place * 8 + k, value, result)
@@ -462,7 +486,7 @@
     for number in range(SUBS):
         advance = [states[c][4] * (number + 1) for c in range(CAP)]
         guesses = [predict(*states[c][0:5]) for c in range(CAP)]
-        inner = near_field([x + v for x, v in guesses], advance)
+        inner = near_field([x + v for x, v in guesses], number)
         after = []
         for c in range(CAP):
             x, v, pull, change, substep, regular, rest = states[c]
@@ -489,10 +513,7 @@
     shifted = mine
     for place in range(1, ACT):
         shifted = jnp.where(sub == place, pltpu.roll(mine, LANES - 32 * place, 1), shifted)
-    columns = jnp.transpose(shifted)
-    o_state[...] = columns[0:6, 0:ACT]
-    o_fields[...] = columns[6:18, 0:ACT]
-    o_taylor[...] = columns[18:24, 0:ACT]
+    o_all[...] = shifted[0:ACT, :]
 
     for copy in first + second + third + fifth + sixth:
         copy.wait_send()
@@ -506,6 +527,12 @@
     def _():
         for copy in down:
             copy.wait_send()
+
+
+def cut(result, state, fields, taylor):
+    state[...] = result[:, 0:6]
+    fields[...] = result[:, 6:18]
+    taylor[...] = result[:, 18:24]
 
 
 def shards(
@@ -532,20 +559,16 @@
     ilanded = pltpu.VMEM((SRC * ROWS, LANES), jnp.int32)
     three = pltpu.VMEM((3, window), jnp.float32)
     one = pltpu.VMEM((1, window), jnp.float32)
-    predicted = pltpu.VMEM((3, stars), jnp.float32)
     dma = pltpu.SemaphoreType.DMA
-    return pl.pallas_call(
+    result = pl.pallas_call(
         kernel,
-        out_shape=(
-            jax.ShapeDtypeStruct((6, ACT), jnp.float32),
-            jax.ShapeDtypeStruct((12, ACT), jnp.float32),
-            jax.ShapeDtypeStruct((6, ACT), jnp.float32),
-        ),
+        out_shape=jax.ShapeDtypeStruct((ACT, LANES), jnp.float32),
         in_specs=[hbm] * 6 + [smem] * 3 + [vmem],
-        out_specs=(vmem, vmem, vmem),
+        out_specs=vmem,
         scratch_shapes=[
-            three, three, three, three, one, one, predicted, predicted,
+            three, three, three, three, one, one, three, three,
             pltpu.VMEM((window // BLOCK, CAP, ROWS, LANES), jnp.float32),
+            pltpu.VMEM((SUBS, window // BLOCK, CAP, 6, ROWS, LANES), jnp.float32),
             itile, ilanded, tile, landed, tile, groups, groups, groups, tile, landed, tile, landed,
             dma((6,)), dma((2, 6)), dma((2, 6)), dma((4, SRC)), dma((4, SRC)),
             dma((TGT,)), dma((TGT,)), dma((TGT,)), dma((TGT,)),
@@ -563,6 +586,17 @@
         counts,
         block_lists,
     )
+    state, fields, taylor = pl.pallas_call(
+        cut,
+        out_shape=(
+            jax.ShapeDtypeStruct((ACT, 6), jnp.float32),
+            jax.ShapeDtypeStruct((ACT, 12), jnp.float32),
+            jax.ShapeDtypeStruct((ACT, 6), jnp.float32),
+        ),
+        in_specs=[vmem],
+        out_specs=(vmem, vmem, vmem),
+    )(result)
+    return state.T, fields.T, taylor.T
 
 
 def solution(mesh):

time: 54.7 us -> 49.6 us (0.907)
  local copies, waits for them, and re-layouts: 2.68 us -> 0 us
  Pallas kernels: 51.2 us -> 48.8 us
    pallas_call x3 -> x0, local copies, waits for them, and re-layouts: 2.66 us -> none  [shards(): pl.pallas_call(kernel, out_shape=(jax.ShapeDtypeStruct((6, ACT), jnp.floa...]
    pallas_call x1 -> x2, Pallas kernels: 51.2 us -> 48.8 us  [the longest x1 47.5 us: shards(): pl.pallas_call(kernel, out_shape=jax.ShapeDtypeStruct((ACT, LANES), jnp.f...]
where the time goes in v2:
time: 49.6 us; the launch traced here: 49.4 us
  Pallas kernels  48.8 us (98%)
  between operations  0.64 us (1%)
    pallas_call x1, Pallas kernels, shards(): pl.pallas_call(kernel, out_shape=jax.ShapeDtypeStruct((ACT, LANES), jnp.f...  47.5 us
    pallas_call x1, Pallas kernels, shards(): pl.pallas_call(cut, out_shape=(jax.ShapeDtypeStruct((ACT, 6), jnp.float32...  1.32 us

profile of v2, /device:TPU:0, one launch (start us, length us, event | category | flops | bytes accessed | tf_op | source)
XLA Modules:
  0.0 49.4 jit_solution(15400977213973491665)
XLA Ops:
  0.6 47.5 %shard_map.121.result = f32[4,128]{1,0:T(4,128)} custom-call(f32[3,4096]{1,0:T(4,128)} %pos.1, f32[3,4096]{1,0:T(4,128)} %vel.1, f32[3,4096]{1,0:T(4,128)} %acc.1, f32[3,4096]{1,0:T(4,128)} %jrk.1, f32[1,4096]{1,0:T(1,128)} %bitcast.5, f32[1,4096]{1,0:T(1,128)} %bitcast.6, s32[4]{0:T(128)} %idx.1, s32[4]{0:T(128)} %own.1, s32[4]{0:T(128)} %cnt.1, s32[4,16]{1,0:T(4,128)} %lists.1), custom_call_target="tpu_custom_call" | custom-call | tf_op jit(solution)/shard_map/pallas_call | solution.py:563
  48.1 1.3 %shard_map.122 = (f32[4,6]{1,0:T(4,128)}, f32[4,12]{1,0:T(4,128)}, f32[4,6]{1,0:T(4,128)}) custom-call(f32[4,128]{1,0:T(4,128)} %shard_map.121.result), custom_call_target="tpu_custom_call" | custom-call | tf_op jit(solution)/shard_map/pallas_call | solution.py:589

commit v3 on v2

--- a/solution.py
+++ b/solution.py
@@ -15,10 +15,12 @@
 SRC = 8
 TGT = 16
 SOFTENING = 0.0001
+PIECES = 4
+UNROLL = 8
 MESH = pl.DeviceIdType.MESH
-PAIRS = ((1, 0), (2, 0), (1, 1), (2, 1), (3, 1), (0, 1), (3, 0), (0, 0))
-DX_TABLE = sum(dx * 4**at for at, (dx, dz) in enumerate(PAIRS))
-DZ_TABLE = sum(dz * 2**at for at, (dx, dz) in enumerate(PAIRS))
+PAIRS = ((0, 1), (1, 1), (2, 0), (3, 0), (2, 1), (3, 1), (1, 0), (0, 0))
+CODE_TABLE = sum(code * 4**at for at, (code, dz) in enumerate(PAIRS))
+DZ_TABLE = sum(dz * 2**at for at, (code, dz) in enumerate(PAIRS))
 
 
 def predict(position, velocity, acceleration, jerk_now, interval):
@@ -75,6 +77,11 @@
     return jnp.broadcast_to(tile[:, lane : lane + 1], (ROWS, LANES))
 
 
+def wide_row(ref, row, block, many):
+    lanes = pl.ds(pl.multiple_of(block * LANES, LANES), LANES)
+    return jnp.broadcast_to(ref[row : row + 1, lanes], (many * ACT * ROWS, LANES))
+
+
 def row_of(ref, row, block):
     lanes = pl.ds(pl.multiple_of(block * LANES, LANES), LANES)
     return jnp.broadcast_to(ref[row : row + 1, lanes], (ROWS, LANES))
@@ -83,9 +90,10 @@
 def kernel(
     pos, vel, acc, jrk, mas, ela, idx, own, cnt, lists,
     o_all,
-    wpos, wvel, wacc, wjrk, wmas, wela, ppos, pvel, mw, moved,
+    wpos, wvel, wacc, wjrk, wmas, wela, ppos, pvel, feat, mw, moved,
     s1b, s1r, s2b, s2r, s3b, s3r, s4b, s4r, s5b, s5r, s6b, s6r,
-    load_sem, halo_send, halo_recv, src_send, src_recv, tgt_send, tgt_recv, sum_send, sum_recv,
+    hsend, hland, idx_here, own_here, cnt_here, lists_here,
+    load_sem, number_sem, halo_send, halo_recv, src_send, src_recv, tgt_send, tgt_recv, sum_send, sum_recv,
 ):
     stars = pos.shape[1]
     blocks = stars // BLOCK
@@ -97,8 +105,9 @@
     def src_peer(step):
         return {"src": lax.rem(me + step, SRC)}
 
-    def tgt_peer(dx, dz, dc):
-        x, z, core = lax.rem(my_x + dx, 4), lax.rem(my_z + dz, 2), lax.rem(my_core + dc, 2)
+    def tgt_peer(code, dz, dc):
+        x = lax.rem(my_x + code * (1 + 2 * lax.rem(my_x, 2)), 4)
+        z, core = lax.rem(my_z + dz, 2), lax.rem(my_core + dc, 2)
         return {"tgt": x * 4 + z * 2 + core}
 
     def tile_rows(at):
@@ -107,6 +116,24 @@
     lane = lax.broadcasted_iota(jnp.int32, (ROWS, LANES), 1)
     sub = lax.broadcasted_iota(jnp.int32, (ROWS, LANES), 0)
     zero = jnp.zeros((ROWS, LANES), jnp.float32)
+
+    barrier = pltpu.get_barrier_semaphore()
+    for step in (4, 3, 5, 2, 6, 1, 7):
+        pl.semaphore_signal(barrier, inc=1, device_id=src_peer(step), device_id_type=MESH)
+    for code, dz in PAIRS:
+        for dc in (1, 0):
+            if code or dz or dc:
+                pl.semaphore_signal(
+                    barrier, inc=1, device_id=tgt_peer(code, dz, dc), device_id_type=MESH
+                )
+
+    numbered = ((idx, idx_here), (own, own_here), (cnt, cnt_here), (lists, lists_here))
+    number_loads = [
+        pltpu.make_async_copy(hbm, here, number_sem.at[at])
+        for at, (hbm, here) in enumerate(numbered)
+    ]
+    for load in number_loads:
+        load.start()
 
     arrays = ((pos, wpos), (vel, wvel), (acc, wacc), (jrk, wjrk), (mas, wmas), (ela, wela))
     loads = [
@@ -115,92 +142,85 @@
     ]
     for load in loads:
         load.start()
-
-    barrier = pltpu.get_barrier_semaphore()
-    for step in range(1, SRC):
-        pl.semaphore_signal(barrier, inc=1, device_id=src_peer(step), device_id_type=MESH)
-    for at in range(1, TGT):
-        pl.semaphore_signal(
-            barrier,
-            inc=1,
-            device_id=tgt_peer(at // 4, (at // 2) % 2, at % 2),
-            device_id_type=MESH,
-        )
+    for load in number_loads:
+        load.wait()
 
     tile = jnp.zeros((ROWS, LANES), jnp.int32)
     for place in range(ACT):
-        for at, ref in enumerate((idx, own, cnt)):
+        for at, ref in enumerate((idx_here, own_here, cnt_here)):
             tile = jnp.where((sub == place) & (lane == 16 + at), ref[place], tile)
     s1b[...] = tile
-    s1b[0:ACT, 0:16] = lists[...]
+    s1b[0:ACT, 0:16] = lists_here[...]
 
     pl.semaphore_wait(barrier, SRC + TGT - 2)
 
     def share(stage, sent, landed):
-        copies = []
-        for step in range(1, SRC):
-            copies.append(
-                pltpu.make_async_remote_copy(
-                    src_ref=sent,
-                    dst_ref=landed.at[tile_rows(me), :],
-                    send_sem=src_send.at[stage, step],
-                    recv_sem=src_recv.at[stage, step],
-                    device_id=src_peer(step),
-                    device_id_type=MESH,
-                )
-            )
-        for copy in copies:
-            copy.start()
-        return copies
+        for step in (4, 3, 5, 2, 6, 1, 7):
+            pltpu.make_async_remote_copy(
+                src_ref=sent,
+                dst_ref=landed.at[tile_rows(me), :],
+                send_sem=src_send.at[stage],
+                recv_sem=src_recv.at[stage],
+                device_id=src_peer(step),
+                device_id_type=MESH,
+            ).start()
+        return stage, landed
+
+    def wait_bytes(ref, semaphore):
+        pltpu.make_async_copy(ref, ref, semaphore).wait()
+
+    def wait_sent(shared):
+        stage, landed = shared
+        wait_bytes(landed.at[0 : (SRC - 1) * ROWS], src_send.at[stage])
+
+    def wait_landed(shared):
+        stage, landed = shared
+        wait_bytes(landed.at[0 : (SRC - 1) * ROWS], src_recv.at[stage])
 
     first = share(0, s1b, s1r)
     s1r[tile_rows(me), :] = s1b[...]
 
-    up = [
-        pltpu.make_async_remote_copy(
-            src_ref=hbm.at[:, stars - HALO : stars],
-            dst_ref=win.at[:, 0:HALO],
-            send_sem=halo_send.at[0, at],
-            recv_sem=halo_recv.at[0, at],
-            device_id={"src": lax.rem(me + 1, SRC)},
-            device_id_type=MESH,
-        )
-        for at, (hbm, win) in enumerate(arrays)
-    ]
-    down = [
-        pltpu.make_async_remote_copy(
-            src_ref=hbm.at[:, 0:HALO],
-            dst_ref=win.at[:, HALO + stars : 2 * HALO + stars],
-            send_sem=halo_send.at[1, at],
-            recv_sem=halo_recv.at[1, at],
-            device_id={"src": lax.rem(me + SRC - 1, SRC)},
-            device_id_type=MESH,
-        )
-        for at, (hbm, win) in enumerate(arrays)
-    ]
-
-    @pl.when(me < SRC - 1)
-    def _():
-        for copy in up:
-            copy.start()
-
-    @pl.when(me > 0)
-    def _():
-        for copy in down:
-            copy.start()
-
-    @pl.when(me == 0)
-    def _():
-        for hbm, win in arrays:
-            win[:, 0:HALO] = jnp.zeros((win.shape[0], HALO), jnp.float32)
-
-    @pl.when(me == SRC - 1)
-    def _():
-        for hbm, win in arrays:
-            win[:, HALO + stars :] = jnp.zeros((win.shape[0], HALO), jnp.float32)
-
     for load in loads:
         load.wait()
+
+    up = pltpu.make_async_remote_copy(
+        src_ref=hsend.at[0],
+        dst_ref=hland.at[0],
+        send_sem=halo_send.at[0],
+        recv_sem=halo_recv.at[0],
+        device_id={"src": lax.rem(me + 1, SRC)},
+        device_id_type=MESH,
+    )
+    down = pltpu.make_async_remote_copy(
+        src_ref=hsend.at[1],
+        dst_ref=hland.at[1],
+        send_sem=halo_send.at[1],
+        recv_sem=halo_recv.at[1],
+        device_id={"src": lax.rem(me + SRC - 1, SRC)},
+        device_id_type=MESH,
+    )
+    row = 0
+    for hbm, win in arrays:
+        height = win.shape[0]
+        hsend[0, row : row + height] = win[:, stars : stars + HALO]
+        hsend[1, row : row + height] = win[:, HALO : 2 * HALO]
+        row += height
+
+    @pl.when(me < SRC - 1)
+    def _():
+        up.start()
+
+    @pl.when(me > 0)
+    def _():
+        down.start()
+
+    @pl.when(me == 0)
+    def _():
+        hland[0] = jnp.zeros(hland.shape[1:], jnp.float32)
+
+    @pl.when(me == SRC - 1)
+    def _():
+        hland[1] = jnp.zeros(hland.shape[1:], jnp.float32)
 
     chunk = 4 * LANES
 
@@ -215,8 +235,27 @@
 
     lax.fori_loop(1, 1 + stars // chunk, predict_chunk, 0)
 
-    for copy in first:
-        copy.wait_recv()
+    def feature_chunk(at, carry):
+        there = pl.ds(pl.multiple_of(HALO + at * chunk, LANES), chunk)
+        wide = lax.broadcasted_iota(jnp.int32, (ROWS, chunk), 0)
+        rest = jnp.where(wide == 6, 1.0, 0.0)
+        for k in range(3):
+            rest = jnp.where(wide == k, jnp.broadcast_to(ppos[k : k + 1, there], (ROWS, chunk)), rest)
+            rest = jnp.where(
+                wide == 3 + k, jnp.broadcast_to(pvel[k : k + 1, there], (ROWS, chunk)), rest
+            )
+        parts = []
+        for part in range(3):
+            parts.append(rest.astype(jnp.bfloat16).astype(jnp.float32))
+            rest = rest - parts[-1]
+        parts.append(jnp.zeros((ROWS, chunk), jnp.float32))
+        here = pl.ds(pl.multiple_of(at * chunk, LANES), chunk)
+        feat[:, here] = jnp.concatenate(parts, 0).astype(jnp.bfloat16)
+        return carry
+
+    lax.fori_loop(0, stars // chunk, feature_chunk, 0)
+
+    wait_landed(first)
 
     numbers = [s1r[pl.ds(place, SRC, stride=ROWS), :] for place in range(ACT)]
     chosen = [[], []]
@@ -281,6 +320,7 @@
     second = share(1, s2b, s2r)
     s2r[tile_rows(me), :] = s2b[...]
 
+    wait_sent(first)
     raw = extract((wpos, wvel, wacc, wjrk, wela))
 
     def mask_block(block, carry):
@@ -294,18 +334,22 @@
 
     @pl.when(me > 0)
     def _():
-        for copy in up:
-            copy.wait_recv()
+        up.wait_recv()
 
     @pl.when(me < SRC - 1)
     def _():
-        for copy in down:
-            copy.wait_recv()
+        down.wait_recv()
+
+    row = 0
+    for hbm, win in arrays:
+        height = win.shape[0]
+        win[:, 0:HALO] = hland[0, row : row + height]
+        win[:, HALO + stars :] = hland[1, row : row + height]
+        row += height
 
     lax.fori_loop(0, window_blocks, mask_block, 0, unroll=4)
 
-    for copy in second:
-        copy.wait_recv()
+    wait_landed(second)
 
     def gathered(ref):
         total = ref[0:ROWS, :]
@@ -316,24 +360,17 @@
     group_targets = gathered(s2r)
     s3b[...] = group_targets
     s3r[0] = group_targets
-    third = []
-    for dx, dz in PAIRS:
+    for code, dz in PAIRS:
         for dc in (1, 0):
-            if (dx, dz, dc) == (0, 0, 0):
-                continue
-            there = ((4 - dx) % 4) * 4 + dz * 2 + dc
-            third.append(
+            if code or dz or dc:
                 pltpu.make_async_remote_copy(
                     src_ref=s3b,
-                    dst_ref=s3r.at[there],
-                    send_sem=tgt_send.at[there],
-                    recv_sem=tgt_recv.at[there],
-                    device_id=tgt_peer(dx, dz, dc),
+                    dst_ref=s3r.at[code * 4 + dz * 2 + dc],
+                    send_sem=tgt_send,
+                    recv_sem=tgt_recv.at[code * 2 + dz],
+                    device_id=tgt_peer(code, dz, dc),
                     device_id_type=MESH,
-                )
-            )
-    for copy in third:
-        copy.start()
+                ).start()
 
     def advance_block(block, carry):
         x = [row_of(wpos, k, block) for k in range(3)]
@@ -372,89 +409,111 @@
     predict_chunk(window_blocks * LANES // chunk - 1, 0)
     inner = near_field(start, None)
 
-    def field(targets):
-        result = zero
-        for half in range(2):
-            places = (2 * half, 2 * half + 1)
-            aims = [[lane_of(targets, place * 8 + k) for k in range(6)] for place in places]
-
-            def step(block, sums):
-                source = [row_of(ppos, k, block) for k in range(3)]
-                source += [row_of(pvel, k, block) for k in range(3)]
-                mass = row_of(wmas, 0, block)
-                return [pair_sums(sums[at], aims[at], source, mass) for at in range(2)]
-
-            sums = lax.fori_loop(
-                HALO // BLOCK,
-                HALO // BLOCK + blocks,
-                step,
-                [[zero] * 9 for _ in range(2)],
-                unroll=8,
+    def field(tiles):
+        many = len(tiles)
+        aims = [
+            jnp.concatenate(
+                [lane_of(tile, place * 8 + k) for tile in tiles for place in range(ACT)], 0
             )
-            for at, place in enumerate(places):
-                for k, value in enumerate(total_of(sums[at])):
-                    result = jnp.where(lane == place * 8 + k, value, result)
-        return result
-
-    def sum_copy(at, dx, dz, dc):
-        there = lax.rem(4 - dx, 4) * 4 + dz * 2 + dc
-        return pltpu.make_async_remote_copy(
-            src_ref=s4b.at[at],
-            dst_ref=s4r.at[there],
-            send_sem=sum_send.at[at],
-            recv_sem=sum_recv.at[there],
-            device_id=tgt_peer(dx, dz, dc),
-            device_id_type=MESH,
+            for k in range(6)
+        ]
+
+        def halves(value):
+            high = value.astype(jnp.bfloat16)
+            return high, (value - high.astype(jnp.float32)).astype(jnp.bfloat16)
+
+        def step(at, sums):
+            columns = []
+            for piece in range(PIECES):
+                block = at * PIECES + piece
+                rows = [wide_row(ppos, k, block + HALO // BLOCK, many) for k in range(3)]
+                rows += [wide_row(pvel, k, block + HALO // BLOCK, many) for k in range(3)]
+                mass = wide_row(wmas, 0, block + HALO // BLOCK, many)
+                u = [rows[k] - aims[k] for k in range(3)]
+                e = [rows[3 + k] - aims[3 + k] for k in range(3)]
+                inverse = lax.rsqrt(u[0] * u[0] + u[1] * u[1] + (u[2] * u[2] + SOFTENING))
+                square = inverse * inverse
+                weight = (mass * inverse) * square
+                radial = weight * ((u[0] * e[0] + u[1] * e[1] + u[2] * e[2]) * square)
+                columns.append(jnp.concatenate(halves(weight) + halves(radial), 0))
+            left = jnp.concatenate(columns, 1)
+            right = feat[:, pl.ds(pl.multiple_of(at * PIECES * LANES, LANES), PIECES * LANES)]
+            return sums + lax.dot_general(
+                left, right, (((1,), (1,)), ((), ())), preferred_element_type=jnp.float32
+            )
+
+        sums = lax.fori_loop(
+            0,
+            blocks // PIECES,
+            step,
+            jnp.zeros((4 * many * ACT * ROWS, 4 * ROWS), jnp.float32),
+            unroll=UNROLL,
         )
-
-    def group_pair(pair, tables):
-        dx, dz = lax.rem(tables[0], 4), lax.rem(tables[1], 2)
-        for dc in (1, 0):
-            at = dx * 4 + dz * 2 + dc
-
-            def wait():
-                pltpu.make_async_remote_copy(
-                    src_ref=s3b,
-                    dst_ref=s3r.at[at],
-                    send_sem=tgt_send.at[at],
-                    recv_sem=tgt_recv.at[at],
-                    device_id=tgt_peer(dx, dz, dc),
-                    device_id_type=MESH,
-                ).wait_recv()
-
-            if dc:
-                wait()
-            else:
-                pl.when(pair < len(PAIRS) - 1)(wait)
-            result = field(s3r[at])
-
-            def send():
-                s4b[at] = result
-                sum_copy(at, dx, dz, dc).start()
-
-            if dc:
-                send()
-            else:
-                pl.when(pair < len(PAIRS) - 1)(send)
-
-                @pl.when(pair == len(PAIRS) - 1)
-                def _():
-                    s4r[0] = result
-
-        return tables[0] // 4, tables[1] // 2
-
-    lax.fori_loop(0, len(PAIRS), group_pair, (jnp.int32(DX_TABLE), jnp.int32(DZ_TABLE)))
-
-    for at in range(1, TGT):
-        sum_copy(at, at // 4, (at // 2) % 2, at % 2).wait_send()
+        blank = jnp.zeros((4 * many * ACT * ROWS, LANES - 4 * ROWS), jnp.float32)
+        sums = jnp.concatenate([sums, blank], 1)
+        results = []
+        for at, targets in enumerate(tiles):
+            result = zero
+            for place in range(ACT):
+                sides = []
+                for array in range(2):
+                    row = (2 * array * ACT * many + at * ACT + place) * ROWS
+                    both = sums[row : row + ROWS] + sums[row + many * ACT * ROWS : row + (many * ACT + 1) * ROWS]
+                    sides.append(
+                        both + pltpu.roll(both, LANES - 8, 1) + pltpu.roll(both, LANES - 16, 1)
+                    )
+                aim = pltpu.roll(targets, (LANES - 8 * place) % LANES, 1) if place else targets
+                plain = sides[0] - aim * lane_of(sides[0], 6)
+                along = sides[1] - aim * lane_of(sides[1], 6)
+                change = plain - 3.0 * pltpu.roll(along, 3, 1)
+                six = jnp.where(lane < 3, plain, change)
+                if place:
+                    six = pltpu.roll(six, 8 * place, 1)
+                result = jnp.where(lane // 8 == place, six, result)
+            results.append(result)
+        return results
+
+    def send_sum(at, code, dz, dc):
         pltpu.make_async_remote_copy(
             src_ref=s4b.at[at],
             dst_ref=s4r.at[at],
-            send_sem=sum_send.at[at],
-            recv_sem=sum_recv.at[at],
-            device_id=tgt_peer(at // 4, (at // 2) % 2, at % 2),
+            send_sem=sum_send,
+            recv_sem=sum_recv,
+            device_id=tgt_peer(code, dz, dc),
             device_id_type=MESH,
-        ).wait_recv()
+        ).start()
+
+    def group_pair(pair, tables):
+        code, dz = lax.rem(tables[0], 4), lax.rem(tables[1], 2)
+        other = pair < len(PAIRS) - 1
+        places = [code * 4 + dz * 2 + dc for dc in (0, 1)]
+
+        @pl.when(other)
+        def _():
+            wait_bytes(s3r.at[pl.ds(0, 2)], tgt_recv.at[code * 2 + dz])
+
+        @pl.when(jnp.logical_not(other))
+        def _():
+            wait_bytes(s3r.at[0], tgt_recv.at[code * 2 + dz])
+
+        results = field([s3r[place] for place in places])
+        for dc in (1, 0):
+            s4b[places[dc]] = results[dc]
+        send_sum(places[1], code, dz, 1)
+
+        @pl.when(other)
+        def _():
+            send_sum(places[0], code, dz, 0)
+
+        @pl.when(jnp.logical_not(other))
+        def _():
+            s4r[0] = results[0]
+
+        return tables[0] // 4, tables[1] // 2
+
+    lax.fori_loop(0, len(PAIRS), group_pair, (jnp.int32(CODE_TABLE), jnp.int32(DZ_TABLE)))
+
+    wait_bytes(s4r.at[pl.ds(0, TGT - 1)], sum_recv)
     group_sum = s4r[0]
     for at in range(1, TGT):
         group_sum = group_sum + s4r[at]
@@ -462,8 +521,20 @@
     s5b[...] = group_sum
     fifth = share(2, s5b, s5r)
     s5r[tile_rows(me), :] = group_sum
-    for copy in fifth:
-        copy.wait_recv()
+    wait_sent(second)
+    wait_bytes(s3r.at[pl.ds(0, TGT - 1)], tgt_send)
+    wait_bytes(s4r.at[pl.ds(0, TGT - 1)], sum_send)
+
+    @pl.when(me < SRC - 1)
+    def _():
+        up.wait_send()
+
+    @pl.when(me > 0)
+    def _():
+        down.wait_send()
+
+    wait_sent(fifth)
+    wait_landed(fifth)
     summed = gathered(s5r)
     lanes_of = [[lane_of(summed, place * 8 + k) for place in range(ACT)] for k in range(6)]
 
@@ -506,8 +577,7 @@
     s6b[...] = spread(results, 32)
     sixth = share(3, s6b, s6r)
     s6r[tile_rows(me), :] = s6b[...]
-    for copy in sixth:
-        copy.wait_recv()
+    wait_landed(sixth)
     mine = jnp.sum(s6r[pl.ds(me, SRC, stride=ROWS), :], axis=0, keepdims=True)
     mine = jnp.broadcast_to(mine, (ROWS, LANES))
     shifted = mine
@@ -515,18 +585,7 @@
         shifted = jnp.where(sub == place, pltpu.roll(mine, LANES - 32 * place, 1), shifted)
     o_all[...] = shifted[0:ACT, :]
 
-    for copy in first + second + third + fifth + sixth:
-        copy.wait_send()
-
-    @pl.when(me < SRC - 1)
-    def _():
-        for copy in up:
-            copy.wait_send()
-
-    @pl.when(me > 0)
-    def _():
-        for copy in down:
-            copy.wait_send()
+    wait_sent(sixth)
 
 
 def cut(result, state, fields, taylor):
@@ -550,7 +609,6 @@
     stars = positions.shape[1]
     window = stars + 2 * HALO
     hbm = pl.BlockSpec(memory_space=pl.ANY)
-    smem = pl.BlockSpec(memory_space=pltpu.SMEM)
     vmem = pl.BlockSpec(memory_space=pltpu.VMEM)
     tile = pltpu.VMEM((ROWS, LANES), jnp.float32)
     landed = pltpu.VMEM((SRC * ROWS, LANES), jnp.float32)
@@ -563,15 +621,19 @@
     result = pl.pallas_call(
         kernel,
         out_shape=jax.ShapeDtypeStruct((ACT, LANES), jnp.float32),
-        in_specs=[hbm] * 6 + [smem] * 3 + [vmem],
+        in_specs=[hbm] * 10,
         out_specs=vmem,
         scratch_shapes=[
             three, three, three, three, one, one, three, three,
+            pltpu.VMEM((4 * ROWS, stars), jnp.bfloat16),
             pltpu.VMEM((window // BLOCK, CAP, ROWS, LANES), jnp.float32),
             pltpu.VMEM((SUBS, window // BLOCK, CAP, 6, ROWS, LANES), jnp.float32),
             itile, ilanded, tile, landed, tile, groups, groups, groups, tile, landed, tile, landed,
-            dma((6,)), dma((2, 6)), dma((2, 6)), dma((4, SRC)), dma((4, SRC)),
-            dma((TGT,)), dma((TGT,)), dma((TGT,)), dma((TGT,)),
+            pltpu.VMEM((2, 14, HALO), jnp.float32), pltpu.VMEM((2, 14, HALO), jnp.float32),
+            pltpu.SMEM((ACT,), jnp.int32), pltpu.SMEM((ACT,), jnp.int32), pltpu.SMEM((ACT,), jnp.int32),
+            pltpu.VMEM((ACT, 16), jnp.int32),
+            dma((6,)), dma((4,)), dma((2,)), dma((2,)), dma((4,)), dma((4,)),
+            dma, dma((len(PAIRS),)), dma, dma,
         ],
         compiler_params=pltpu.CompilerParams(collective_id=0, has_side_effects=True),
     )(

time: 49.6 us -> 45.7 us (0.921)
  Pallas kernels: 48.8 us -> 44.8 us
    pallas_call x1, Pallas kernels: 47.5 us -> 43.5 us  [shards(): pl.pallas_call(kernel, out_shape=jax.ShapeDtypeStruct((ACT, LANES), jnp.f...]
where the time goes in v3:
time: 45.7 us; the launch traced here: 45.5 us
  Pallas kernels  44.8 us (98%)
  between operations  0.64 us (1%)
    pallas_call x1, Pallas kernels, shards(): pl.pallas_call(kernel, out_shape=jax.ShapeDtypeStruct((ACT, LANES), jnp.f...  43.5 us
    pallas_call x1, Pallas kernels, shards(): pl.pallas_call(cut, out_shape=(jax.ShapeDtypeStruct((ACT, 6), jnp.float32...  1.32 us

profile of v3, /device:TPU:0, one launch (start us, length us, event | category | flops | bytes accessed | tf_op | source)
XLA Modules:
  0.0 45.5 jit_solution(17561604845499826464)
XLA Ops:
  0.6 43.5 %shard_map.121.result = f32[4,128]{1,0:T(4,128)} custom-call(f32[3,4096]{1,0:T(4,128)} %pos.1, f32[3,4096]{1,0:T(4,128)} %vel.1, f32[3,4096]{1,0:T(4,128)} %acc.1, f32[3,4096]{1,0:T(4,128)} %jrk.1, f32[1,4096]{1,0:T(1,128)} %bitcast.5, f32[1,4096]{1,0:T(1,128)} %bitcast.6, s32[4]{0:T(128)} %idx.1, s32[4]{0:T(128)} %own.1, s32[4]{0:T(128)} %cnt.1, s32[4,16]{1,0:T(4,128)} %lists.1), custom_call_target="tpu_custom_call" | custom-call | tf_op jit(solution)/shard_map/pallas_call | solution.py:621
  44.2 1.3 %shard_map.122 = (f32[4,6]{1,0:T(4,128)}, f32[4,12]{1,0:T(4,128)}, f32[4,6]{1,0:T(4,128)}) custom-call(f32[4,128]{1,0:T(4,128)} %shard_map.121.result), custom_call_target="tpu_custom_call" | custom-call | tf_op jit(solution)/shard_map/pallas_call | solution.py:651

commit v4 on v3

--- a/solution.py
+++ b/solution.py
@@ -452,25 +452,14 @@
         blank = jnp.zeros((4 * many * ACT * ROWS, LANES - 4 * ROWS), jnp.float32)
         sums = jnp.concatenate([sums, blank], 1)
         results = []
-        for at, targets in enumerate(tiles):
-            result = zero
-            for place in range(ACT):
-                sides = []
-                for array in range(2):
-                    row = (2 * array * ACT * many + at * ACT + place) * ROWS
-                    both = sums[row : row + ROWS] + sums[row + many * ACT * ROWS : row + (many * ACT + 1) * ROWS]
-                    sides.append(
-                        both + pltpu.roll(both, LANES - 8, 1) + pltpu.roll(both, LANES - 16, 1)
-                    )
-                aim = pltpu.roll(targets, (LANES - 8 * place) % LANES, 1) if place else targets
-                plain = sides[0] - aim * lane_of(sides[0], 6)
-                along = sides[1] - aim * lane_of(sides[1], 6)
-                change = plain - 3.0 * pltpu.roll(along, 3, 1)
-                six = jnp.where(lane < 3, plain, change)
-                if place:
-                    six = pltpu.roll(six, 8 * place, 1)
-                result = jnp.where(lane // 8 == place, six, result)
-            results.append(result)
+        for at in range(many):
+            for array in range(2):
+                tile = zero
+                for place in range(ACT):
+                    row = ((2 * array * many + at) * ACT + place) * ROWS
+                    both = sums[row : row + ROWS] + sums[row + many * ACT * ROWS :][0:ROWS]
+                    tile = tile + (pltpu.roll(both, 32 * place, 1) if place else both)
+                results.append(tile)
         return results
 
     def send_sum(at, code, dz, dc):
@@ -498,7 +487,8 @@
 
         results = field([s3r[place] for place in places])
         for dc in (1, 0):
-            s4b[places[dc]] = results[dc]
+            for array in range(2):
+                s4b[places[dc], array] = results[2 * dc + array]
         send_sum(places[1], code, dz, 1)
 
         @pl.when(other)
@@ -507,16 +497,30 @@
 
         @pl.when(jnp.logical_not(other))
         def _():
-            s4r[0] = results[0]
+            for array in range(2):
+                s4r[0, array] = results[array]
 
         return tables[0] // 4, tables[1] // 2
 
     lax.fori_loop(0, len(PAIRS), group_pair, (jnp.int32(CODE_TABLE), jnp.int32(DZ_TABLE)))
 
+    aim = group_targets
+    for place in range(1, ACT):
+        aim = jnp.where(lane // 32 == place, pltpu.roll(group_targets, 24 * place, 1), aim)
     wait_bytes(s4r.at[pl.ds(0, TGT - 1)], sum_recv)
-    group_sum = s4r[0]
-    for at in range(1, TGT):
-        group_sum = group_sum + s4r[at]
+    sides = []
+    for array in range(2):
+        both = s4r[0, array]
+        for at in range(1, TGT):
+            both = both + s4r[at, array]
+        both = both + pltpu.roll(both, LANES - 8, 1) + pltpu.roll(both, LANES - 16, 1)
+        ones = lane_of(both, 6)
+        for place in range(1, ACT):
+            ones = jnp.where(lane // 32 == place, lane_of(both, 32 * place + 6), ones)
+        sides.append(both - aim * ones)
+    group_sum = jnp.where(
+        lax.rem(lane, 32) < 3, sides[0], sides[0] - 3.0 * pltpu.roll(sides[1], 3, 1)
+    )
 
     s5b[...] = group_sum
     fifth = share(2, s5b, s5r)
@@ -536,7 +540,7 @@
     wait_sent(fifth)
     wait_landed(fifth)
     summed = gathered(s5r)
-    lanes_of = [[lane_of(summed, place * 8 + k) for place in range(ACT)] for k in range(6)]
+    lanes_of = [[lane_of(summed, place * 32 + k) for place in range(ACT)] for k in range(6)]
 
     totals = [[pick(c, lanes_of[k], zero) for k in range(6)] for c in range(CAP)]
     states = []
@@ -613,6 +617,7 @@
     tile = pltpu.VMEM((ROWS, LANES), jnp.float32)
     landed = pltpu.VMEM((SRC * ROWS, LANES), jnp.float32)
     groups = pltpu.VMEM((TGT, ROWS, LANES), jnp.float32)
+    sums = pltpu.VMEM((TGT, 2, ROWS, LANES), jnp.float32)
     itile = pltpu.VMEM((ROWS, LANES), jnp.int32)
     ilanded = pltpu.VMEM((SRC * ROWS, LANES), jnp.int32)
     three = pltpu.VMEM((3, window), jnp.float32)
@@ -620,7 +625,7 @@
     dma = pltpu.SemaphoreType.DMA
     result = pl.pallas_call(
         kernel,
-        out_shape=jax.ShapeDtypeStruct((ACT, LANES), jnp.float32),
+        out_shape=pltpu.VMEM((ACT, LANES), jnp.float32),
         in_specs=[hbm] * 10,
         out_specs=vmem,
         scratch_shapes=[
@@ -628,7 +633,7 @@
             pltpu.VMEM((4 * ROWS, stars), jnp.bfloat16),
             pltpu.VMEM((window // BLOCK, CAP, ROWS, LANES), jnp.float32),
             pltpu.VMEM((SUBS, window // BLOCK, CAP, 6, ROWS, LANES), jnp.float32),
-            itile, ilanded, tile, landed, tile, groups, groups, groups, tile, landed, tile, landed,
+            itile, ilanded, tile, landed, tile, groups, sums, sums, tile, landed, tile, landed,
             pltpu.VMEM((2, 14, HALO), jnp.float32), pltpu.VMEM((2, 14, HALO), jnp.float32),
             pltpu.SMEM((ACT,), jnp.int32), pltpu.SMEM((ACT,), jnp.int32), pltpu.SMEM((ACT,), jnp.int32),
             pltpu.VMEM((ACT, 16), jnp.int32),
@@ -657,7 +662,7 @@
         ),
         in_specs=[vmem],
         out_specs=(vmem, vmem, vmem),
-    )(result)
+    )(pltpu.with_memory_space_constraint(result, pltpu.VMEM))
     return state.T, fields.T, taylor.T
 
 

time: 45.7 us -> 43.4 us (0.950)
  Pallas kernels: 44.8 us -> 42.6 us
    pallas_call x1, Pallas kernels: 43.5 us -> 42 us  [shards(): pl.pallas_call(kernel, out_shape=pltpu.VMEM((ACT, LANES), jnp.float32), i...]
    pallas_call x1, Pallas kernels: 1.32 us -> 0.65 us  [shards(): pl.pallas_call(cut, out_shape=(jax.ShapeDtypeStruct((ACT, 6), jnp.float32...]
where the time goes in v4:
time: 43.4 us; the launch traced here: 43.3 us
  Pallas kernels  42.6 us (98%)
  between operations  0.64 us (1%)
    pallas_call x1, Pallas kernels, shards(): pl.pallas_call(kernel, out_shape=pltpu.VMEM((ACT, LANES), jnp.float32), i...  42 us

profile of v4, /device:TPU:0, one launch (start us, length us, event | category | flops | bytes accessed | tf_op | source)
XLA Modules:
  0.0 43.3 jit_solution(15697904431329422179)
XLA Ops:
  0.6 42.0 %shard_map.121.result = f32[4,128]{1,0:T(4,128)S(1)} custom-call(f32[3,4096]{1,0:T(4,128)} %pos.1, f32[3,4096]{1,0:T(4,128)} %vel.1, f32[3,4096]{1,0:T(4,128)} %acc.1, f32[3,4096]{1,0:T(4,128)} %jrk.1, f32[1,4096]{1,0:T(1,128)} %bitcast.5, f32[1,4096]{1,0:T(1,128)} %bitcast.6, s32[4]{0:T(128)} %idx.1, s32[4]{0:T(128)} %own.1, s32[4]{0:T(128)} %cnt.1, ...), custom_call_target="tpu_custom_call" | custom-call | tf_op jit(solution)/shard_map/pallas_call | solution.py:626
  42.6 0.7 %shard_map.122 = (f32[4,6]{1,0:T(4,128)}, f32[4,12]{1,0:T(4,128)}, f32[4,6]{1,0:T(4,128)}) custom-call(f32[4,128]{1,0:T(4,128)S(1)} %shard_map.121.result), custom_call_target="tpu_custom_call" | custom-call | tf_op jit(solution)/shard_map/pallas_call | solution.py:656

commit v5 on v4

--- a/solution.py
+++ b/solution.py
@@ -18,9 +18,13 @@
 PIECES = 4
 UNROLL = 8
 MESH = pl.DeviceIdType.MESH
-PAIRS = ((0, 1), (1, 1), (2, 0), (3, 0), (2, 1), (3, 1), (1, 0), (0, 0))
-CODE_TABLE = sum(code * 4**at for at, (code, dz) in enumerate(PAIRS))
-DZ_TABLE = sum(dz * 2**at for at, (code, dz) in enumerate(PAIRS))
+ORDERS = (
+    ((0, 0), (1, 0), (2, 0), (3, 0), (2, 1), (3, 1), (1, 1), (0, 1)),
+    ((0, 1), (2, 1), (3, 1), (2, 0), (3, 0), (1, 1), (1, 0), (0, 0)),
+)
+CODE_TABLES = [sum(code * 4**at for at, (code, dz) in enumerate(order)) for order in ORDERS]
+DZ_TABLES = [sum(dz * 2**at for at, (code, dz) in enumerate(order)) for order in ORDERS]
+PAIRS = ORDERS[1]
 
 
 def predict(position, velocity, acceleration, jerk_now, interval):
@@ -238,12 +242,12 @@
     def feature_chunk(at, carry):
         there = pl.ds(pl.multiple_of(HALO + at * chunk, LANES), chunk)
         wide = lax.broadcasted_iota(jnp.int32, (ROWS, chunk), 0)
-        rest = jnp.where(wide == 6, 1.0, 0.0)
+        mass = jnp.broadcast_to(wmas[:, there], (ROWS, chunk))
+        rest = jnp.where(wide == 6, mass, 0.0)
         for k in range(3):
-            rest = jnp.where(wide == k, jnp.broadcast_to(ppos[k : k + 1, there], (ROWS, chunk)), rest)
-            rest = jnp.where(
-                wide == 3 + k, jnp.broadcast_to(pvel[k : k + 1, there], (ROWS, chunk)), rest
-            )
+            x = jnp.broadcast_to(ppos[k : k + 1, there], (ROWS, chunk))
+            v = jnp.broadcast_to(pvel[k : k + 1, there], (ROWS, chunk))
+            rest = jnp.where(wide == k, mass * x, jnp.where(wide == 3 + k, mass * v, rest))
         parts = []
         for part in range(3):
             parts.append(rest.astype(jnp.bfloat16).astype(jnp.float32))
@@ -428,12 +432,11 @@
                 block = at * PIECES + piece
                 rows = [wide_row(ppos, k, block + HALO // BLOCK, many) for k in range(3)]
                 rows += [wide_row(pvel, k, block + HALO // BLOCK, many) for k in range(3)]
-                mass = wide_row(wmas, 0, block + HALO // BLOCK, many)
                 u = [rows[k] - aims[k] for k in range(3)]
                 e = [rows[3 + k] - aims[3 + k] for k in range(3)]
                 inverse = lax.rsqrt(u[0] * u[0] + u[1] * u[1] + (u[2] * u[2] + SOFTENING))
                 square = inverse * inverse
-                weight = (mass * inverse) * square
+                weight = inverse * square
                 radial = weight * ((u[0] * e[0] + u[1] * e[1] + u[2] * e[2]) * square)
                 columns.append(jnp.concatenate(halves(weight) + halves(radial), 0))
             left = jnp.concatenate(columns, 1)
@@ -474,7 +477,7 @@
 
     def group_pair(pair, tables):
         code, dz = lax.rem(tables[0], 4), lax.rem(tables[1], 2)
-        other = pair < len(PAIRS) - 1
+        other = code + dz > 0
         places = [code * 4 + dz * 2 + dc for dc in (0, 1)]
 
         @pl.when(other)
@@ -500,9 +503,10 @@
             for array in range(2):
                 s4r[0, array] = results[array]
 
-        return tables[0] // 4, tables[1] // 2
-
-    lax.fori_loop(0, len(PAIRS), group_pair, (jnp.int32(CODE_TABLE), jnp.int32(DZ_TABLE)))
+        return [lax.div(tables[0], 4), lax.div(tables[1], 2)]
+
+    tables = [low + my_z * (high - low) for low, high in (CODE_TABLES, DZ_TABLES)]
+    lax.fori_loop(0, len(PAIRS), group_pair, tables)
 
     aim = group_targets
     for place in range(1, ACT):

time: 43.4 us -> 42.4 us (0.977)
  Pallas kernels: 42.6 us -> 41.6 us
    pallas_call x1, Pallas kernels: 42 us -> 41 us  [shards(): pl.pallas_call(kernel, out_shape=pltpu.VMEM((ACT, LANES), jnp.float32), i...]
where the time goes in v5:
time: 42.4 us; the launch traced here: 42.3 us
  Pallas kernels  41.6 us (98%)
  between operations  0.64 us (2%)
    pallas_call x1, Pallas kernels, shards(): pl.pallas_call(kernel, out_shape=pltpu.VMEM((ACT, LANES), jnp.float32), i...  41 us

profile of v5, /device:TPU:0, one launch (start us, length us, event | category | flops | bytes accessed | tf_op | source)
XLA Modules:
  0.0 42.3 jit_solution(3269696428158010171)
XLA Ops:
  0.6 41.0 %shard_map.121.result = f32[4,128]{1,0:T(4,128)S(1)} custom-call(f32[3,4096]{1,0:T(4,128)} %pos.1, f32[3,4096]{1,0:T(4,128)} %vel.1, f32[3,4096]{1,0:T(4,128)} %acc.1, f32[3,4096]{1,0:T(4,128)} %jrk.1, f32[1,4096]{1,0:T(1,128)} %bitcast.5, f32[1,4096]{1,0:T(1,128)} %bitcast.6, s32[4]{0:T(128)} %idx.1, s32[4]{0:T(128)} %own.1, s32[4]{0:T(128)} %cnt.1, ...), custom_call_target="tpu_custom_call" | custom-call | tf_op jit(solution)/shard_map/pallas_call | solution.py:630
  41.6 0.7 %shard_map.122 = (f32[4,6]{1,0:T(4,128)}, f32[4,12]{1,0:T(4,128)}, f32[4,6]{1,0:T(4,128)}) custom-call(f32[4,128]{1,0:T(4,128)S(1)} %shard_map.121.result), custom_call_target="tpu_custom_call" | custom-call | tf_op jit(solution)/shard_map/pallas_call | solution.py:660

commit v6 on v5

--- a/solution.py
+++ b/solution.py
@@ -20,7 +20,7 @@
 MESH = pl.DeviceIdType.MESH
 ORDERS = (
     ((0, 0), (1, 0), (2, 0), (3, 0), (2, 1), (3, 1), (1, 1), (0, 1)),
-    ((0, 1), (2, 1), (3, 1), (2, 0), (3, 0), (1, 1), (1, 0), (0, 0)),
+    ((0, 1), (1, 1), (2, 1), (3, 1), (2, 0), (3, 0), (1, 0), (0, 0)),
 )
 CODE_TABLES = [sum(code * 4**at for at, (code, dz) in enumerate(order)) for order in ORDERS]
 DZ_TABLES = [sum(dz * 2**at for at, (code, dz) in enumerate(order)) for order in ORDERS]
@@ -295,7 +295,7 @@
                 out.append([jnp.where(here, row, old) for row, old in zip(rows, found[c])])
             return out
 
-        found = lax.fori_loop(0, blocks, step, [[zero] * wide for _ in range(CAP)], unroll=2)
+        found = lax.fori_loop(0, blocks, step, [[zero] * wide for _ in range(CAP)], unroll=8)
         return [
             [
                 jnp.broadcast_to(jnp.sum(part, axis=1, keepdims=True), (ROWS, LANES))
@@ -352,29 +352,6 @@
         row += height
 
     lax.fori_loop(0, window_blocks, mask_block, 0, unroll=4)
-
-    wait_landed(second)
-
-    def gathered(ref):
-        total = ref[0:ROWS, :]
-        for at in range(1, SRC):
-            total = total + ref[at * ROWS : (at + 1) * ROWS, :]
-        return total
-
-    group_targets = gathered(s2r)
-    s3b[...] = group_targets
-    s3r[0] = group_targets
-    for code, dz in PAIRS:
-        for dc in (1, 0):
-            if code or dz or dc:
-                pltpu.make_async_remote_copy(
-                    src_ref=s3b,
-                    dst_ref=s3r.at[code * 4 + dz * 2 + dc],
-                    send_sem=tgt_send,
-                    recv_sem=tgt_recv.at[code * 2 + dz],
-                    device_id=tgt_peer(code, dz, dc),
-                    device_id_type=MESH,
-                ).start()
 
     def advance_block(block, carry):
         x = [row_of(wpos, k, block) for k in range(3)]
@@ -412,6 +389,29 @@
     predict_chunk(0, 0)
     predict_chunk(window_blocks * LANES // chunk - 1, 0)
     inner = near_field(start, None)
+
+    wait_landed(second)
+
+    def gathered(ref):
+        total = ref[0:ROWS, :]
+        for at in range(1, SRC):
+            total = total + ref[at * ROWS : (at + 1) * ROWS, :]
+        return total
+
+    group_targets = gathered(s2r)
+    s3b[...] = group_targets
+    s3r[0] = group_targets
+    for code, dz in PAIRS:
+        for dc in (1, 0):
+            if code or dz or dc:
+                pltpu.make_async_remote_copy(
+                    src_ref=s3b,
+                    dst_ref=s3r.at[code * 4 + dz * 2 + dc],
+                    send_sem=tgt_send,
+                    recv_sem=tgt_recv.at[code * 2 + dz],
+                    device_id=tgt_peer(code, dz, dc),
+                    device_id_type=MESH,
+                ).start()
 
     def field(tiles):
         many = len(tiles)

time: 42.4 us -> 40.8 us (0.962)
  the two profiles are of different devices: /device:TPU:0 before, /device:TPU:64 now
where the time goes in v6:
time: 40.8 us; the launch traced here: 40.6 us
  Pallas kernels  40 us (98%)
  between operations  0.64 us (2%)
    pallas_call x1, Pallas kernels, shards(): pl.pallas_call(kernel, out_shape=pltpu.VMEM((ACT, LANES), jnp.float32), i...  39.3 us

profile of v6, /device:TPU:64, one launch (start us, length us, event | category | flops | bytes accessed | tf_op | source)
XLA Modules:
  0.0 40.6 jit_solution(15450590753323475140)
XLA Ops:
  0.6 39.3 %shard_map.121.result = f32[4,128]{1,0:T(4,128)S(1)} custom-call(f32[3,4096]{1,0:T(4,128)} %pos.1, f32[3,4096]{1,0:T(4,128)} %vel.1, f32[3,4096]{1,0:T(4,128)} %acc.1, f32[3,4096]{1,0:T(4,128)} %jrk.1, f32[1,4096]{1,0:T(1,128)} %bitcast.5, f32[1,4096]{1,0:T(1,128)} %bitcast.6, s32[4]{0:T(128)} %idx.1, s32[4]{0:T(128)} %own.1, s32[4]{0:T(128)} %cnt.1, ...), custom_call_target="tpu_custom_call" | custom-call | tf_op jit(solution)/shard_map/pallas_call | solution.py:630
  40.0 0.7 %shard_map.122 = (f32[4,6]{1,0:T(4,128)}, f32[4,12]{1,0:T(4,128)}, f32[4,6]{1,0:T(4,128)}) custom-call(f32[4,128]{1,0:T(4,128)S(1)} %shard_map.121.result), custom_call_target="tpu_custom_call" | custom-call | tf_op jit(solution)/shard_map/pallas_call | solution.py:660

commit v7 on v6

--- a/solution.py
+++ b/solution.py
@@ -383,7 +383,7 @@
                 sources = [[moved[number, block, c, k] for k in range(6)] for c in range(CAP)]
             return [pair_sums(sums[c], targets[c], sources[c], mw[block, c]) for c in range(CAP)]
 
-        sums = lax.fori_loop(0, window_blocks, step, [[zero] * 9 for _ in range(CAP)], unroll=8)
+        sums = lax.fori_loop(0, window_blocks, step, [[zero] * 9 for _ in range(CAP)], unroll=True)
         return [total_of(sums[c]) for c in range(CAP)]
 
     predict_chunk(0, 0)

time: 40.8 us -> 40.7 us (level)
  no operation moved by 1% of the time
where the time goes in v7:
time: 40.7 us; the launch traced here: 40.5 us
  Pallas kernels  39.9 us (98%)
  between operations  0.64 us (2%)
    pallas_call x1, Pallas kernels, shards(): pl.pallas_call(kernel, out_shape=pltpu.VMEM((ACT, LANES), jnp.float32), i...  39.2 us

profile of v7, /device:TPU:64, one launch (start us, length us, event | category | flops | bytes accessed | tf_op | source)
XLA Modules:
  0.0 40.5 jit_solution(17936444949933715080)
XLA Ops:
  0.6 39.2 %shard_map.121.result = f32[4,128]{1,0:T(4,128)S(1)} custom-call(f32[3,4096]{1,0:T(4,128)} %pos.1, f32[3,4096]{1,0:T(4,128)} %vel.1, f32[3,4096]{1,0:T(4,128)} %acc.1, f32[3,4096]{1,0:T(4,128)} %jrk.1, f32[1,4096]{1,0:T(1,128)} %bitcast.5, f32[1,4096]{1,0:T(1,128)} %bitcast.6, s32[4]{0:T(128)} %idx.1, s32[4]{0:T(128)} %own.1, s32[4]{0:T(128)} %cnt.1, ...), custom_call_target="tpu_custom_call" | custom-call | tf_op jit(solution)/shard_map/pallas_call | solution.py:630
  39.9 0.7 %shard_map.122 = (f32[4,6]{1,0:T(4,128)}, f32[4,12]{1,0:T(4,128)}, f32[4,6]{1,0:T(4,128)}) custom-call(f32[4,128]{1,0:T(4,128)S(1)} %shard_map.121.result), custom_call_target="tpu_custom_call" | custom-call | tf_op jit(solution)/shard_map/pallas_call | solution.py:660

commit v8 on v7

--- a/solution.py
+++ b/solution.py
@@ -20,7 +20,7 @@
 MESH = pl.DeviceIdType.MESH
 ORDERS = (
     ((0, 0), (1, 0), (2, 0), (3, 0), (2, 1), (3, 1), (1, 1), (0, 1)),
-    ((0, 1), (1, 1), (2, 1), (3, 1), (2, 0), (3, 0), (1, 0), (0, 0)),
+    ((0, 1), (1, 1), (3, 1), (2, 1), (3, 0), (2, 0), (1, 0), (0, 0)),
 )
 CODE_TABLES = [sum(code * 4**at for at, (code, dz) in enumerate(order)) for order in ORDERS]
 DZ_TABLES = [sum(dz * 2**at for at, (code, dz) in enumerate(order)) for order in ORDERS]

time: 40.7 us -> 40.7 us (level)
  no operation moved by 1% of the time
where the time goes in v8:
time: 40.7 us; the launch traced here: 40.5 us
  Pallas kernels  39.9 us (98%)
  between operations  0.64 us (2%)
    pallas_call x1, Pallas kernels, shards(): pl.pallas_call(kernel, out_shape=pltpu.VMEM((ACT, LANES), jnp.float32), i...  39.2 us

profile of v8, /device:TPU:64, one launch (start us, length us, event | category | flops | bytes accessed | tf_op | source)
XLA Modules:
  0.0 40.5 jit_solution(190074894504362606)
XLA Ops:
  0.6 39.2 %shard_map.121.result = f32[4,128]{1,0:T(4,128)S(1)} custom-call(f32[3,4096]{1,0:T(4,128)} %pos.1, f32[3,4096]{1,0:T(4,128)} %vel.1, f32[3,4096]{1,0:T(4,128)} %acc.1, f32[3,4096]{1,0:T(4,128)} %jrk.1, f32[1,4096]{1,0:T(1,128)} %bitcast.5, f32[1,4096]{1,0:T(1,128)} %bitcast.6, s32[4]{0:T(128)} %idx.1, s32[4]{0:T(128)} %own.1, s32[4]{0:T(128)} %cnt.1, ...), custom_call_target="tpu_custom_call" | custom-call | tf_op jit(solution)/shard_map/pallas_call | solution.py:630
  39.9 0.7 %shard_map.122 = (f32[4,6]{1,0:T(4,128)}, f32[4,12]{1,0:T(4,128)}, f32[4,6]{1,0:T(4,128)}) custom-call(f32[4,128]{1,0:T(4,128)S(1)} %shard_map.121.result), custom_call_target="tpu_custom_call" | custom-call | tf_op jit(solution)/shard_map/pallas_call | solution.py:660
